TPU v7x, 512 devices: a whole 4x4x16 slice. The times are simulated.
512 devices in a mesh: ctx: 64 (over z, y), head: 8 (over x, core).
Axes of the slice: x: 4, y: 4, z: 16, core: 2. Of those that a mesh axis runs over, the one named last changes fastest.
Arguments:
- queries: bfloat16 [16384, 4096], P('ctx', 'head'), may hold values from -6 to 6
- keys: bfloat16 [16384, 4096], P('ctx', 'head'), may hold values from -6 to 6
- values: bfloat16 [16384, 4096], P('ctx', 'head'), may hold values from -70 to 70
- d_out: bfloat16 [16384, 4096], P('ctx', 'head'), may hold values from -6 to 6
- gain: float32 [4096], P('head'), may hold values from 0.25 to 1.75
- live_rows: int32 [64], P('ctx'), may hold values from 64 to 256, as said below
- doc_start: int32 [16384], P('ctx'), may hold values from 0 to 1, as said below
Outputs:
- normed: bfloat16 [16384, 4096], P('ctx', 'head')
- grad_queries: bfloat16 [16384, 4096], P('ctx', 'head')
- grad_keys: bfloat16 [16384, 4096], P('ctx', 'head')
- grad_values: bfloat16 [16384, 4096], P('ctx', 'head')
- grad_gain: float32 [4096], P('head')
Inputs may be any that keep to these rules, and one draw needn't show every extreme that they name: `live_rows`: some block is full in every draw. `doc_start`: flags on rows that are not live are ignored.
All inputs are finite; a program needn't handle non-finite values.
Results may differ from a plain program's by a relative error of at most 0.0052.
Values sent between devices are 32-bit elements; how exact they have to be, the bound alone decides.
A program may use at most 64 MiB of HBM per device.

v0:
```python
import jax
import jax.numpy as jnp
from jax import lax
from jax.sharding import PartitionSpec as P

HEADS = 32
HEAD_DIM = 128


epsilon = 1e-06


def carried_in(shard, axis, combine, identity, reverse):
    count, index = (lax.axis_size(axis), lax.axis_index(axis))
    everything = jax.tree.map(lambda part: lax.all_gather(part, axis), shard)
    start = jax.tree.map(
        lambda part, zero: jnp.broadcast_to(jnp.asarray(zero, part.dtype), part.shape),
        shard,
        identity,
    )

    def lap(k, before):
        at = count - 1 - k if reverse else k
        reached = at > index if reverse else at < index
        new = combine(before, jax.tree.map(lambda part: part[at], everything))
        return jax.tree.map(lambda a, b: jnp.where(reached, a, b), new, before)

    return lax.fori_loop(0, count, lap, start)


def combine(earlier, later):
    return (later[0] + (1.0 - later[1]) * earlier[0], jnp.maximum(earlier[1], later[1]))


def split_state(state):
    upper = lax.optimization_barrier(state.astype(jnp.bfloat16))
    lower = (state - upper.astype(jnp.float32)).astype(jnp.bfloat16)
    return (upper, lower)


def state_product(formula, operand, parts):
    first = jnp.einsum(formula, operand, parts[0], preferred_element_type=jnp.float32)
    return first + jnp.einsum(formula, operand, parts[1], preferred_element_type=jnp.float32)


def per_device(queries, keys, values, d_out, gain, live_rows, doc_start):
    row_count = queries.shape[0]
    head_shape = (row_count, -1, HEAD_DIM)
    query_heads = queries.reshape(head_shape)
    key_heads = keys.reshape(head_shape)
    value_heads = values.reshape(head_shape)
    local_heads = query_heads.shape[1]
    slot_index = jnp.arange(row_count, dtype=jnp.int32)
    live_mask = slot_index < live_rows[0]
    start_flags = jnp.where(live_mask, doc_start, 0)
    local_id = jnp.cumsum(start_flags)
    last_doc = local_id[-1]
    has_start = (last_doc > 0).astype(jnp.float32)
    order_ok = slot_index[None, :] <= slot_index[:, None]
    pair_mask = (
        (local_id[:, None] == local_id[None, :])
        & order_ok
        & live_mask[:, None]
        & live_mask[None, :]
    )
    head_rows = (live_mask & (local_id == 0)).astype(jnp.float32)[:, None, None]
    tail_rows = (live_mask & (local_id == last_doc)).astype(jnp.float32)[:, None, None]
    zero_state = jnp.zeros((local_heads, HEAD_DIM, HEAD_DIM), jnp.float32)
    scores = jnp.einsum("thf,shf->hts", query_heads, key_heads, preferred_element_type=jnp.float32)
    weights = jnp.where(pair_mask[None], scores, 0.0).astype(jnp.bfloat16)
    local_part = jnp.einsum(
        "hts,shf->thf", weights, value_heads, preferred_element_type=jnp.float32
    )
    tail_keys = jnp.where(tail_rows > 0, key_heads, jnp.zeros_like(key_heads))
    tail_state = jnp.einsum(
        "thf,thg->hfg", tail_keys, value_heads, preferred_element_type=jnp.float32
    )
    state_in, _ = carried_in(
        (tail_state, has_start), "ctx", combine, (zero_state, jnp.float32(0.0)), False
    )
    forward_parts = split_state(state_in)
    carried = state_product("thf,hfg->thg", query_heads, forward_parts) * head_rows
    attended = (local_part + carried).reshape(row_count, -1)
    upstream = d_out.astype(jnp.float32)
    scaled = gain[None, :] * upstream
    square_sum, inner_sum = lax.psum(
        (jnp.sum(attended * attended, axis=1), jnp.sum(scaled * attended, axis=1)), "head"
    )
    model_width = HEADS * HEAD_DIM
    radius = jnp.sqrt(square_sum / model_width + epsilon)
    normed = (attended / radius[:, None] * gain[None, :]).astype(jnp.bfloat16)
    grad_att = (
        scaled / radius[:, None] - attended * (inner_sum / (model_width * radius**3))[:, None]
    )
    grad_att = jnp.where(live_mask[:, None], grad_att, 0.0).astype(jnp.bfloat16).reshape(head_shape)
    gain_term = jnp.sum(upstream * attended / radius[:, None], axis=0)
    grad_gain = lax.psum(gain_term, "ctx")
    probe_scores = jnp.einsum(
        "thg,shg->hts", grad_att, value_heads, preferred_element_type=jnp.float32
    )
    probe_weights = jnp.where(pair_mask[None], probe_scores, 0.0).astype(jnp.bfloat16)
    grad_query = jnp.einsum(
        "hts,shf->thf", probe_weights, key_heads, preferred_element_type=jnp.float32
    )
    grad_query = grad_query + state_product("thg,hfg->thf", grad_att, forward_parts) * head_rows
    head_queries = jnp.where(head_rows > 0, query_heads, jnp.zeros_like(query_heads))
    head_state = jnp.einsum(
        "thf,thg->hfg", head_queries, grad_att, preferred_element_type=jnp.float32
    )
    state_back, _ = carried_in(
        (head_state, has_start), "ctx", combine, (zero_state, jnp.float32(0.0)), True
    )
    backward_parts = split_state(state_back)
    grad_key = jnp.einsum(
        "hts,thf->shf", probe_weights, query_heads, preferred_element_type=jnp.float32
    )
    grad_key = grad_key + state_product("shg,hfg->shf", value_heads, backward_parts) * tail_rows
    grad_value = jnp.einsum("hts,thg->shg", weights, grad_att, preferred_element_type=jnp.float32)
    grad_value = grad_value + state_product("shf,hfg->shg", key_heads, backward_parts) * tail_rows
    return (
        normed,
        grad_query.reshape(row_count, -1).astype(jnp.bfloat16),
        grad_key.reshape(row_count, -1).astype(jnp.bfloat16),
        grad_value.reshape(row_count, -1).astype(jnp.bfloat16),
        grad_gain,
    )


def solution(mesh):
    return jax.shard_map(
        per_device,
        mesh=mesh,
        in_specs=(
            P("ctx", "head"),
            P("ctx", "head"),
            P("ctx", "head"),
            P("ctx", "head"),
            P("head"),
            P("ctx"),
            P("ctx"),
        ),
        out_specs=(
            P("ctx", "head"),
            P("ctx", "head"),
            P("ctx", "head"),
            P("ctx", "head"),
            P("head"),
        ),
        check_vma=False,
    )
```

profile of v0, /device:TPU:1, one launch (start us, length us, event | category | flops | bytes accessed | tf_op | source)
XLA Modules:
  0.0 748.8 jit_solution(1898766268123108366)
XLA Ops:
  14.3 1.3 dynamic-slice
  16.4 123.7 %all-reduce = f32[64]{0:T(128)S(1)} all-reduce(f32[64]{0:T(128)S(1)} %dynamic-update-slice), channel_id=1, replica_groups=mesh['ctx'=64,'head'=8] {'ctx'}, use_global_device_ids=true, to_apply=%add | all-reduce | flops 64 | bytes 512
  140.2 1.3 fusion.2
  141.8 69.3 %all-gather.5.cloned.1.call-done = f32[256,128,128]{2,1,0:T(8,128)} async-done(((f32[4,128,128]{2,1,0:T(8,128)}), f32[256,128,128]{2,1,0:T(8,128)}) %all-gather.5.cloned.1.call-update) | async-done | bytes 16777232 | tf_op jit(solution)/shard_map/all_gather | solution.py:15
  211.1 154.4 %while.30 = (s32[]{:T(128)}, f32[4,128,128]{2,1,0:T(8,128)S(1)}, s32[]{:T(128)}, f32[64,4,128,128]{3,2,1,0:T(8,128)}, f32[64]{0:T(128)S(1)}, /*index=5*/s32[]{:T(128)}, f32[1]{0:T(128)}, s32[]{:T(128)}) while((s32[]{:T(128)}, f32[4,128,128]{2,1,0:T(8,128)S(1)}, s32[]{:T(128)}, f32[64,4,128,128]{3,2,1,0:T(8,128)}, f32[64]{0:T(128)S(1)}, ...), condition=%wide.region_3.4_spmd.clone, body=%wide.region_2.3_spmd.clone.sunk | while | flops 262149 | bytes 786577 | solution.py:28
  212.3 1.1 fusion.90
  214.8 1.1 fusion.90
  217.2 1.1 fusion.90
  219.6 1.1 fusion.90
  229.2 1.1 fusion.90
  231.6 1.1 fusion.90
  234.1 1.1 fusion.90
  236.5 1.1 fusion.90
  238.9 1.1 fusion.90
  241.3 1.1 fusion.90
  251.0 1.1 fusion.90
  253.4 1.1 fusion.90
  255.8 1.1 fusion.90
  258.2 1.1 fusion.90
  260.6 1.1 fusion.90
  263.0 1.1 fusion.90
  265.4 1.1 fusion.90
  275.1 1.1 fusion.90
  277.5 1.1 fusion.90
  279.9 1.1 fusion.90
  282.3 1.1 fusion.90
  284.7 1.1 fusion.90
  287.2 1.1 fusion.90
  296.8 1.1 fusion.90
  299.2 1.1 fusion.90
  301.6 1.1 fusion.90
  304.0 1.1 fusion.90
  306.5 1.1 fusion.90
  308.9 1.1 fusion.90
  311.3 1.1 fusion.90
  320.9 1.1 fusion.90
  323.3 1.1 fusion.90
  325.8 1.1 fusion.90
  328.2 1.1 fusion.90
  330.6 1.1 fusion.90
  333.0 1.1 fusion.90
  342.7 1.1 fusion.90
  366.4 13.1 %psum.21 = f32[256]{0:T(256)S(1)} all-reduce(f32[256]{0:T(256)S(1)} %get-tuple-element.313), channel_id=1, replica_groups=mesh['ctx'=64,'head'=8] {'head'}, use_global_device_ids=true, to_apply=%region_5.6 | all-reduce | flops 256 | bytes 2048 | tf_op jit(solution)/shard_map/psum | solution.py:86
  380.6 13.9 %psum.22 = f32[256]{0:T(256)S(1)} all-reduce(f32[256]{0:T(256)S(1)} %get-tuple-element.285), channel_id=1, replica_groups=mesh['ctx'=64,'head'=8] {'head'}, use_global_device_ids=true, to_apply=%region_7.8 | all-reduce | flops 256 | bytes 2048 | tf_op jit(solution)/shard_map/psum | solution.py:86
  394.5 1.9 fusion.24
  399.4 113.3 %psum.23 = f32[512]{0:T(512)} all-reduce(f32[512]{0:T(512)S(1)} %get-tuple-element.284), channel_id=1, replica_groups=mesh['ctx'=64,'head'=8] {'ctx'}, use_global_device_ids=true, to_apply=%region_11.12 | all-reduce | flops 512 | bytes 4096 | tf_op jit(solution)/shard_map/psum | solution.py:97
  513.2 71.1 %all-gather.7.cloned.1.call-done = f32[256,128,128]{2,1,0:T(8,128)} async-done(((f32[4,128,128]{2,1,0:T(8,128)}), f32[256,128,128]{2,1,0:T(8,128)}) %all-gather.7.cloned.1.call-update) | async-done | bytes 16777232 | tf_op jit(solution)/shard_map/all_gather | solution.py:15
  584.4 154.9 %while.31 = (s32[]{:T(128)}, f32[4,128,128]{2,1,0:T(8,128)S(1)}, s32[]{:T(128)}, f32[64,4,128,128]{3,2,1,0:T(8,128)}, f32[64]{0:T(128)S(1)}, /*index=5*/s32[]{:T(128)}, s32[]{:T(128)}, s32[]{:T(128)}, s32[]{:T(128)}, f32[1]{0:T(128)}) while((s32[]{:T(128)}, f32[4,128,128]{2,1,0:T(8,128)S(1)}, s32[]{:T(128)}, ...), condition=%wide.region_9.10_spmd.clone, body=%wide.region_8.9_spmd.clone.sunk | while | flops 262153 | bytes 786639 | solution.py:28
  (267 shorter events, 194.8 us)
Async XLA Ops:
  7.2 4.4 copy-start
  7.2 732.3 %copy-start.1 = (bf16[256,512]{1,0:T(8,128)(2,1)S(1)}, bf16[256,512]{1,0:T(8,128)(2,1)}, u32[]{:S(2)}) copy-start(bf16[256,512]{1,0:T(8,128)(2,1)} %param.12) | copy-start | bytes 786436
  7.2 203.9 %all-gather.5.cloned.1.call-start = ((), (), s32[]{:S(2)}) async-start(), calls=%async_computation | async-start | bytes 17039360 | tf_op jit(solution)/shard_map/all_gather | solution.py:15
  12.5 571.8 %all-gather.7.cloned.1.call-start = ((), (), s32[]{:S(2)}) async-start(), calls=%async_computation.1 | async-start | bytes 17039360 | tf_op jit(solution)/shard_map/all_gather | solution.py:15
Sparse Core Ops, SparseCore 0:
  12.6 198.4 all-gather.4
  397.6 186.7 all-gather.6
where the time goes:
time: 754 us; the launch traced here: 749 us
  blocking collectives  264 us (35%)
  other arithmetic  152 us (20%)
  waiting for transfers between devices  140 us (19%)
  loops' own time  87.1 us (12%)
  local copies, waits for them, and re-layouts  82.9 us (11%)
  between operations  15.6 us (2%)
    select_n x128, other arithmetic, lap(): return jax.tree.map(lambda a, b: jnp.where(reached, a, b), new, before)  147 us
    all_gather x2, waiting for transfers between devices, carried_in(): everything = jax.tree.map(lambda part: lax.all_gather(part, axis), shard)  140 us
    unnamed x1, blocking collectives  124 us
    psum x1, blocking collectives, per_device(): grad_gain = lax.psum(gain_term, 'ctx')  113 us
    another operation x2, loops' own time, carried_in(): return lax.fori_loop(0, count, lap, start)  87.1 us
    dynamic_slice x128, local copies, waits for them, and re-layouts, lap(): new = combine(before, jax.tree.map(lambda part: part[at], everything))  75.1 us
    psum x2, blocking collectives, per_device(): lax.psum((jnp.sum(attended * attended, axis=1), jnp.sum(scaled * attended...  27 us
  transfers between devices with their start and end apart: 2, of which 2 were waited for; matrix products, arithmetic and copies ran while one was open for 1% of the time, Pallas kernels for 0%

commit v1 on v0

v1 whole, which is shorter than its diff:
```python
import jax
import jax.numpy as jnp
from jax import lax
from jax.experimental import pallas as pl
from jax.experimental.pallas import tpu as pltpu
from jax.sharding import PartitionSpec as P

HEADS = 32
HEAD_DIM = 128
D = HEADS * HEAD_DIM
EPSILON = 1e-06
ROWS = 256
LOCAL = 4
CUBE = 16
GROUPS = 4
PIECE = 32
HEAD_PEERS = 8
MESH = pl.DeviceIdType.MESH
F32 = jnp.float32
BF16 = jnp.bfloat16


def dot(a, b, ca, cb):
    return lax.dot_general(a, b, (((ca,), (cb,)), ((), ())), preferred_element_type=F32)


def halves(x):
    upper = x.astype(BF16)
    return upper, (x - upper.astype(F32)).astype(BF16)


def kernel(
    q_hbm, k_hbm, v_hbm, y_hbm, gain_ref, live_ref, doc_ref,
    normed_hbm, dq_hbm, dk_hbm, dv_hbm, dgain_ref,
    q_ref, k_ref, v_ref, y_ref,
    mask_ref, w_ref, att_ref, ga_ref, gh_ref, qh_ref, qht_ref, kt_ref, vt_ref,
    normed_ref, dq_ref, dk_ref, dv_ref, dkl_ref, dvl_ref,
    flag_src, flag_buf, keep_buf,
    t_ref, tin_ref, pre_ref, tot_ref, totin_ref, carry_ref, sout_ref, s_ref,
    h_ref, hin_ref, suf_ref, htot_ref, htotin_ref, rout_ref, r_ref,
    ps_src, ps_buf, gg_src, gg_buf, gt_src, gt_buf,
    in_sem, out_sem,
    fs, fr, l1s, l1r, l2s, l2r, l3s, l3r, pss, psr,
    b1s, b1r, b2s, b2r, b3s, b3r, g1s, g1r, g2s, g2r,
):
    c = lax.axis_index("ctx")
    me = lax.axis_index("head")
    p = lax.rem(c, CUBE)
    g = lax.div(c, CUBE)
    base = g * CUBE

    def rank(a):
        return lax.rem(p + a, CUBE)

    barrier = pltpu.get_barrier_semaphore()
    for a in range(1, CUBE):
        pl.semaphore_signal(barrier, inc=1, device_id={"ctx": base + rank(a)}, device_id_type=MESH)
    for b in range(1, GROUPS):
        pl.semaphore_signal(
            barrier, inc=1, device_id={"ctx": lax.rem(g + b, GROUPS) * CUBE + p}, device_id_type=MESH
        )
    for a in range(1, HEAD_PEERS):
        pl.semaphore_signal(
            barrier, inc=1, device_id={"head": lax.rem(me + a, HEAD_PEERS)}, device_id_type=MESH
        )

    loads = [
        pltpu.make_async_copy(src, dst, in_sem.at[i])
        for i, (src, dst) in enumerate(
            ((k_hbm, k_ref), (v_hbm, v_ref), (q_hbm, q_ref), (y_hbm, y_ref))
        )
    ]
    for load in loads:
        load.start()

    def remote(src, dst, send, recv, where):
        return pltpu.make_async_remote_copy(
            src_ref=src, dst_ref=dst, send_sem=send, recv_sem=recv, device_id=where, device_id_type=MESH
        )

    live = live_ref[0]
    lane = lax.broadcasted_iota(jnp.int32, (ROWS, ROWS), 1)
    sub = lax.broadcasted_iota(jnp.int32, (ROWS, ROWS), 0)
    row8 = lax.broadcasted_iota(jnp.int32, (8, ROWS), 1)
    docs = jnp.broadcast_to(doc_ref[...].reshape(1, ROWS), (8, ROWS))
    starts = jnp.where(row8 < live, docs, 0).astype(F32).astype(BF16)
    upto = jnp.where(sub <= lane, 1.0, 0.0).astype(BF16)
    since = jnp.where(lane <= sub, 1.0, 0.0).astype(BF16)
    id_row = dot(starts, upto, 1, 0)[0:1, :]
    id_col = dot(since, starts, 1, 1)[:, 0:1]
    last = id_row[:, ROWS - 1 : ROWS]
    col = lax.broadcasted_iota(jnp.int32, (ROWS, 1), 0)
    live_col = jnp.where(col < live, 1.0, 0.0)
    tail_col = jnp.where(id_col == last, live_col, 0.0)
    head_col = jnp.where(id_col == 0.0, live_col, 0.0)
    flag = jnp.broadcast_to(jnp.where(last > 0.0, 1.0, 0.0), (1, HEAD_DIM))
    flag_src[...] = flag
    flag_buf[p] = flag
    mask_ref[...] = jnp.where((id_col == id_row) & (lane <= sub), live_col, 0.0)
    tail_b = jnp.broadcast_to(tail_col, (ROWS, HEAD_DIM)).astype(BF16)
    head_b = jnp.broadcast_to(head_col, (ROWS, HEAD_DIM)).astype(BF16)
    live_b = jnp.broadcast_to(live_col, (ROWS, HEAD_DIM))

    def cols(h):
        return pl.ds(h * HEAD_DIM, HEAD_DIM)

    loads[0].wait()
    loads[1].wait()
    for h in range(LOCAL):
        kt = k_ref[:, cols(h)] * tail_b
        kt_ref[:, cols(h)] = kt
        t_ref[pl.ds(4 * h, 4)] = dot(kt, v_ref[:, cols(h)], 0, 0).reshape(4, PIECE, HEAD_DIM)
    tin_ref[p] = t_ref[p]

    pl.semaphore_wait(barrier, CUBE - 1 + GROUPS - 1 + HEAD_PEERS - 1)

    flags = [
        remote(flag_src, flag_buf.at[p], fs.at[a], fr.at[a], {"ctx": base + rank(a)}) for a in range(1, CUBE)
    ]
    level1 = [
        remote(t_ref.at[rank(a)], tin_ref.at[p], l1s.at[a], l1r.at[a], {"ctx": base + rank(a)})
        for a in range(1, CUBE)
    ]
    for copy in flags + level1:
        copy.start()

    loads[2].wait()
    for h in range(LOCAL):
        qs = q_ref[:, cols(h)]
        scores = dot(qs, k_ref[:, cols(h)], 1, 1)
        weights = (scores * mask_ref[...]).astype(BF16)
        w_ref[h] = weights
        att_ref[:, cols(h)] = dot(weights, v_ref[:, cols(h)], 1, 0)
        qh = qs * head_b
        qh_ref[:, cols(h)] = qh
        qht_ref[h] = qh.T
        vt_ref[:, cols(h)] = v_ref[:, cols(h)] * tail_b
    loads[3].wait()

    for copy in flags + level1:
        copy.wait_recv()

    acc = jnp.zeros((PIECE, HEAD_DIM), F32)
    keep = jnp.ones((1, HEAD_DIM), F32)
    for i in range(CUBE):
        pre_ref[i] = acc
        keep_buf[i] = keep
        hold = 1.0 - flag_buf[i]
        acc = tin_ref[i] + hold * acc
        keep = keep * hold
    flag_tile = jnp.broadcast_to(1.0 - keep, (8, HEAD_DIM))
    tot_ref[pl.ds(0, PIECE)] = acc
    tot_ref[pl.ds(PIECE, 8)] = flag_tile
    htot_ref[pl.ds(PIECE, 8)] = flag_tile

    def up(b):
        return remote(tot_ref, totin_ref.at[g], l2s.at[b], l2r.at[b], {"ctx": lax.rem(g + b, GROUPS) * CUBE + p})

    for b in range(1, GROUPS):
        @pl.when(g + b < GROUPS)
        def _():
            up(b).start()

    carry_ref[...] = jnp.zeros((PIECE, HEAD_DIM), F32)
    for b in range(GROUPS - 1, 0, -1):
        @pl.when(g - b >= 0)
        def _():
            up(b).wait_recv()
            at = lax.rem(g + GROUPS - b, GROUPS)
            hold = 1.0 - totin_ref[at, pl.ds(PIECE, 1), :]
            carry_ref[...] = totin_ref[at, pl.ds(0, PIECE), :] + hold * carry_ref[...]

    carry = carry_ref[...]
    level3 = []
    for a in range(1, CUBE):
        i = rank(a)
        sout_ref[i] = pre_ref[i] + keep_buf[i] * carry
        copy = remote(sout_ref.at[i], s_ref.at[p], l3s.at[a], l3r.at[a], {"ctx": base + i})
        copy.start()
        level3.append(copy)
    s_ref[p] = pre_ref[p] + keep_buf[p] * carry
    for copy in level3:
        copy.wait_recv()

    square = jnp.zeros((ROWS, HEAD_DIM), F32)
    inner = jnp.zeros((ROWS, HEAD_DIM), F32)
    for h in range(LOCAL):
        upper, lower = halves(s_ref[pl.ds(4 * h, 4)].reshape(HEAD_DIM, HEAD_DIM))
        qh = qh_ref[:, cols(h)]
        att = att_ref[:, cols(h)] + dot(
            jnp.concatenate([qh, qh], axis=1), jnp.concatenate([upper, lower], axis=0), 1, 0
        )
        att_ref[:, cols(h)] = att
        square = square + att * att
        inner = inner + att * (y_ref[:, cols(h)].astype(F32) * gain_ref[pl.ds(h * HEAD_DIM, HEAD_DIM)].reshape(1, HEAD_DIM))
    ones = jnp.ones((8, 2 * HEAD_DIM), BF16)
    sums = [dot(ones, jnp.concatenate(halves(x), axis=1), 1, 1)[0:1, :] for x in (square, inner)]
    sums = jnp.concatenate(sums, axis=1)
    ps_src[...] = sums
    ps_buf[me] = sums
    shared = [
        remote(ps_src, ps_buf.at[me], pss.at[a], psr.at[a], {"head": lax.rem(me + a, HEAD_PEERS)})
        for a in range(1, HEAD_PEERS)
    ]
    for copy in shared:
        copy.start()
    for copy in shared:
        copy.wait_recv()
    sums = ps_buf[0]
    for i in range(1, HEAD_PEERS):
        sums = sums + ps_buf[i]
    inverse = lax.rsqrt(sums[:, :ROWS] / D + EPSILON)
    factor = sums[:, ROWS:] * (inverse * inverse * inverse / D)
    inverse_col = jnp.broadcast_to(inverse, (HEAD_DIM, ROWS)).T
    factor_col = jnp.broadcast_to(factor, (HEAD_DIM, ROWS)).T

    back1 = []
    gain_terms = []
    for h in range(LOCAL):
        att = att_ref[:, cols(h)]
        y = y_ref[:, cols(h)].astype(F32)
        gains = gain_ref[pl.ds(h * HEAD_DIM, HEAD_DIM)].reshape(1, HEAD_DIM)
        ga = ((y * gains) * inverse_col - att * factor_col) * live_b
        ga = ga.astype(BF16)
        ga_ref[:, cols(h)] = ga
        h_ref[pl.ds(4 * h, 4)] = dot(qht_ref[h], ga, 1, 0).reshape(4, PIECE, HEAD_DIM)
    hin_ref[p] = h_ref[p]
    back1 = [
        remote(h_ref.at[rank(a)], hin_ref.at[p], b1s.at[a], b1r.at[a], {"ctx": base + rank(a)})
        for a in range(1, CUBE)
    ]
    for copy in back1:
        copy.start()

    for h in range(LOCAL):
        att = att_ref[:, cols(h)]
        y = y_ref[:, cols(h)].astype(F32)
        gains = gain_ref[pl.ds(h * HEAD_DIM, HEAD_DIM)].reshape(1, HEAD_DIM)
        unit = att * inverse_col
        normed_ref[:, cols(h)] = (unit * gains).astype(BF16)
        gain_terms.append(jnp.sum(y * unit, axis=0, keepdims=True))
    gain_term = jnp.concatenate(gain_terms, axis=1)
    gg_src[...] = gain_term
    gg_buf[p] = gain_term
    gain1 = [
        remote(gg_src, gg_buf.at[p], g1s.at[a], g1r.at[a], {"ctx": base + rank(a)}) for a in range(1, CUBE)
    ]
    for copy in gain1:
        copy.start()
    stores = [
        pltpu.make_async_copy(src, dst, out_sem.at[i])
        for i, (src, dst) in enumerate(
            ((normed_ref, normed_hbm), (dq_ref, dq_hbm), (dk_ref, dk_hbm), (dv_ref, dv_hbm))
        )
    ]
    stores[0].start()
    for h in range(LOCAL):
        ga = ga_ref[:, cols(h)]
        probes = (dot(ga, v_ref[:, cols(h)], 1, 1) * mask_ref[...]).astype(BF16)
        upper, lower = halves(s_ref[pl.ds(4 * h, 4)].reshape(HEAD_DIM, HEAD_DIM))
        gh = ga * head_b
        carried = dot(jnp.concatenate([gh, gh], axis=1), jnp.concatenate([upper, lower], axis=1), 1, 1)
        dq_ref[:, cols(h)] = (dot(probes, k_ref[:, cols(h)], 1, 0) + carried).astype(BF16)
        dkl_ref[:, cols(h)] = dot(probes, q_ref[:, cols(h)], 0, 0)
    stores[1].start()

    for copy in back1:
        copy.wait_recv()
    acc = jnp.zeros((PIECE, HEAD_DIM), F32)
    keep = jnp.ones((1, HEAD_DIM), F32)
    for i in range(CUBE - 1, -1, -1):
        suf_ref[i] = acc
        keep_buf[i] = keep
        hold = 1.0 - flag_buf[i]
        acc = hin_ref[i] + hold * acc
        keep = keep * hold
    htot_ref[pl.ds(0, PIECE)] = acc

    def down(b):
        return remote(
            htot_ref, htotin_ref.at[g], b2s.at[b], b2r.at[b], {"ctx": lax.rem(g + GROUPS - b, GROUPS) * CUBE + p}
        )

    for b in range(1, GROUPS):
        @pl.when(g - b >= 0)
        def _():
            down(b).start()

    for copy in gain1:
        copy.wait_recv()
    total = gg_buf[0]
    for i in range(1, CUBE):
        total = total + gg_buf[i]
    gt_src[...] = total
    gt_buf[g] = total
    gain2 = [
        remote(gt_src, gt_buf.at[g], g2s.at[b], g2r.at[b], {"ctx": lax.rem(g + b, GROUPS) * CUBE + p})
        for b in range(1, GROUPS)
    ]
    for copy in gain2:
        copy.start()

    for h in range(LOCAL):
        dvl_ref[:, cols(h)] = dot(w_ref[h], ga_ref[:, cols(h)], 0, 0)

    carry_ref[...] = jnp.zeros((PIECE, HEAD_DIM), F32)
    for b in range(GROUPS - 1, 0, -1):
        @pl.when(g + b < GROUPS)
        def _():
            down(b).wait_recv()
            at = lax.rem(g + b, GROUPS)
            hold = 1.0 - htotin_ref[at, pl.ds(PIECE, 1), :]
            carry_ref[...] = htotin_ref[at, pl.ds(0, PIECE), :] + hold * carry_ref[...]
    carry = carry_ref[...]
    back3 = []
    for a in range(1, CUBE):
        i = rank(a)
        rout_ref[i] = suf_ref[i] + keep_buf[i] * carry
        copy = remote(rout_ref.at[i], r_ref.at[p], b3s.at[a], b3r.at[a], {"ctx": base + i})
        copy.start()
        back3.append(copy)
    r_ref[p] = suf_ref[p] + keep_buf[p] * carry

    for copy in gain2:
        copy.wait_recv()
    dgain_ref[...] = (((gt_buf[0] + gt_buf[1]) + gt_buf[2]) + gt_buf[3]).reshape(LOCAL * HEAD_DIM)

    for copy in back3:
        copy.wait_recv()
    for h in range(LOCAL):
        upper, lower = halves(r_ref[pl.ds(4 * h, 4)].reshape(HEAD_DIM, HEAD_DIM))
        vt = vt_ref[:, cols(h)]
        kt = kt_ref[:, cols(h)]
        dk = dkl_ref[:, cols(h)] + dot(
            jnp.concatenate([vt, vt], axis=1), jnp.concatenate([upper, lower], axis=1), 1, 1
        )
        dk_ref[:, cols(h)] = dk.astype(BF16)
        dv = dvl_ref[:, cols(h)] + dot(
            jnp.concatenate([kt, kt], axis=1), jnp.concatenate([upper, lower], axis=0), 1, 0
        )
        dv_ref[:, cols(h)] = dv.astype(BF16)
    stores[2].start()
    stores[3].start()
    for copy in flags + level1 + level3 + shared + back1 + gain1 + gain2 + back3:
        copy.wait_send()
    for b in range(1, GROUPS):
        @pl.when(g + b < GROUPS)
        def _():
            up(b).wait_send()

        @pl.when(g - b >= 0)
        def _():
            down(b).wait_send()
    for store in stores:
        store.wait()


def per_device(queries, keys, values, d_out, gain, live_rows, doc_start):
    any_space = pl.BlockSpec(memory_space=pl.ANY)
    vmem = pl.BlockSpec(memory_space=pltpu.VMEM)
    wide = LOCAL * HEAD_DIM
    block = (ROWS, wide)
    pieces = (CUBE, PIECE, HEAD_DIM)
    dma = pltpu.SemaphoreType.DMA
    scratch = [pltpu.VMEM(block, BF16)] * 4
    scratch += [
        pltpu.VMEM((ROWS, ROWS), F32),
        pltpu.VMEM((LOCAL, ROWS, ROWS), BF16),
        pltpu.VMEM(block, F32),
        pltpu.VMEM(block, BF16),
        pltpu.VMEM(block, BF16),
        pltpu.VMEM(block, BF16),
        pltpu.VMEM((LOCAL, HEAD_DIM, ROWS), BF16),
        pltpu.VMEM(block, BF16),
        pltpu.VMEM(block, BF16),
    ]
    scratch += [pltpu.VMEM(block, BF16)] * 4 + [pltpu.VMEM(block, F32)] * 2
    scratch += [
        pltpu.VMEM((1, HEAD_DIM), F32),
        pltpu.VMEM((CUBE, 1, HEAD_DIM), F32),
        pltpu.VMEM((CUBE, 1, HEAD_DIM), F32),
    ]
    total = (PIECE + 8, HEAD_DIM)
    scratch += [
        pltpu.VMEM(pieces, F32),
        pltpu.VMEM(pieces, F32),
        pltpu.VMEM(pieces, F32),
        pltpu.VMEM(total, F32),
        pltpu.VMEM((GROUPS,) + total, F32),
        pltpu.VMEM((PIECE, HEAD_DIM), F32),
        pltpu.VMEM(pieces, F32),
        pltpu.VMEM(pieces, F32),
    ]
    scratch += [
        pltpu.VMEM(pieces, F32),
        pltpu.VMEM(pieces, F32),
        pltpu.VMEM(pieces, F32),
        pltpu.VMEM(total, F32),
        pltpu.VMEM((GROUPS,) + total, F32),
        pltpu.VMEM(pieces, F32),
        pltpu.VMEM(pieces, F32),
    ]
    scratch += [
        pltpu.VMEM((1, 2 * ROWS), F32),
        pltpu.VMEM((HEAD_PEERS, 1, 2 * ROWS), F32),
        pltpu.VMEM((1, wide), F32),
        pltpu.VMEM((CUBE, 1, wide), F32),
        pltpu.VMEM((1, wide), F32),
        pltpu.VMEM((GROUPS, 1, wide), F32),
    ]
    scratch += [dma((4,)), dma((4,))]
    for count in (CUBE, CUBE, GROUPS, CUBE, HEAD_PEERS, CUBE, GROUPS, CUBE, CUBE, GROUPS):
        scratch += [dma((count,)), dma((count,))]
    shape = jax.ShapeDtypeStruct(block, BF16)
    return pl.pallas_call(
        kernel,
        out_shape=(shape, shape, shape, shape, jax.ShapeDtypeStruct((wide,), F32)),
        in_specs=[any_space] * 4 + [vmem, pl.BlockSpec(memory_space=pltpu.SMEM), vmem],
        out_specs=(any_space,) * 4 + (vmem,),
        scratch_shapes=scratch,
        compiler_params=pltpu.CompilerParams(
            collective_id=0, has_side_effects=True, vmem_limit_bytes=40 * 1024 * 1024
        ),
    )(queries, keys, values, d_out, gain, live_rows, doc_start)


def solution(mesh):
    block = P("ctx", "head")
    return jax.shard_map(
        per_device,
        mesh=mesh,
        in_specs=(block, block, block, block, P("head"), P("ctx"), P("ctx")),
        out_specs=(block, block, block, block, P("head")),
        check_vma=False,
    )
```

time: 754 us -> 78.3 us (0.10)
  blocking collectives: 264 us -> 0 us
  other arithmetic: 152 us -> 0 us
  waiting for transfers between devices: 140 us -> 0 us
  loops' own time: 87.1 us -> 0 us
  local copies, waits for them, and re-layouts: 82.9 us -> 7.88 us
  Pallas kernels: 0 us -> 68.4 us
  between operations: 15.6 us -> 1.32 us
    select_n x128 -> x0, other arithmetic: 147 us -> none  [lap(): return jax.tree.map(lambda a, b: jnp.where(reached, a, b), new, before)]
    all_gather x2 -> x0, waiting for transfers between devices: 140 us -> none  [carried_in(): everything = jax.tree.map(lambda part: lax.all_gather(part, axis), shard)]
    psum x3 -> x0, blocking collectives: 140 us -> none  [the longest x1 113 us: per_device(): grad_gain = lax.psum(gain_term, 'ctx')]
    unnamed x1 -> x0, blocking collectives: 124 us -> none
    another operation x2 -> x0, loops' own time: 87.1 us -> none  [carried_in(): return lax.fori_loop(0, count, lap, start)]
    dynamic_slice x128 -> x0, local copies, waits for them, and re-layouts: 75.1 us -> none  [lap(): new = combine(before, jax.tree.map(lambda part: part[at], everything))]
    pallas_call x0 -> x1, Pallas kernels: none -> 68.4 us  [per_device(): pl.pallas_call(kernel, out_shape=(shape, shape, shape, shape, jax.ShapeDt...]
  transfers between devices with their start and end apart: 2 -> 0, of which waited for: 2 -> 0; matrix products, arithmetic and copies ran while one was open for 1% -> 0% of each run, Pallas kernels for 0% -> 0%
where the time goes in v1:
time: 78.3 us; the launch traced here: 77.6 us
  Pallas kernels  68.4 us (87%)
  local copies, waits for them, and re-layouts  7.88 us (10%)
  between operations  1.32 us (2%)
    pallas_call x1, Pallas kernels, per_device(): pl.pallas_call(kernel, out_shape=(shape, shape, shape, shape, jax.ShapeDt...  68.4 us
    unnamed x17, local copies, waits for them, and re-layouts  7.88 us

profile of v1, /device:TPU:1, one launch (start us, length us, event | category | flops | bytes accessed | tf_op | source)
XLA Modules:
  0.0 77.6 jit_solution(15768359614240665342)
XLA Ops:
  0.6 0.0 copy-start.5
  1.3 0.0 copy-done.5
  1.3 0.0 copy-start
  1.3 0.9 %copy-done = bf16[256,512]{1,0:T(8,128)(2,1)S(1)} copy-done((bf16[256,512]{1,0:T(8,128)(2,1)S(1)}, bf16[256,512]{1,0:T(8,128)(2,1)}, u32[]{:S(2)}) %copy-start) | copy-done | bytes 262168
  2.3 0.0 copy-start.1
  2.3 0.9 %copy-done.1 = bf16[256,512]{1,0:T(8,128)(2,1)S(1)} copy-done((bf16[256,512]{1,0:T(8,128)(2,1)S(1)}, bf16[256,512]{1,0:T(8,128)(2,1)}, u32[]{:S(2)}) %copy-start.1) | copy-done | bytes 262168
  3.2 0.0 copy-start.2
  3.2 0.9 %copy-done.2 = bf16[256,512]{1,0:T(8,128)(2,1)S(1)} copy-done((bf16[256,512]{1,0:T(8,128)(2,1)S(1)}, bf16[256,512]{1,0:T(8,128)(2,1)}, u32[]{:S(2)}) %copy-start.2) | copy-done | bytes 262168
  4.2 0.0 copy-start.3
  4.2 0.9 %copy-done.3 = bf16[256,512]{1,0:T(8,128)(2,1)S(1)} copy-done((bf16[256,512]{1,0:T(8,128)(2,1)S(1)}, bf16[256,512]{1,0:T(8,128)(2,1)}, u32[]{:S(2)}) %copy-start.3) | copy-done | bytes 262168
  5.1 0.0 copy-start.4
  5.1 0.7 copy-done.4
  5.8 68.4 %shard_map.110 = (bf16[256,512]{1,0:T(8,128)(2,1)S(1)}, bf16[256,512]{1,0:T(8,128)(2,1)S(1)}, bf16[256,512]{1,0:T(8,128)(2,1)S(1)}, bf16[256,512]{1,0:T(8,128)(2,1)S(1)}, f32[512]{0:T(512)S(1)}) custom-call(bf16[256,512]{1,0:T(8,128)(2,1)S(1)} %copy-done, bf16[256,512]{1,0:T(8,128)(2,1)S(1)} %copy-done.1, bf16[256,512]{1,0:T(8,128)(2,1)S(1)} %copy-done.2, ...), custom_call_target="tpu_custom_call" | custom-call | tf_op jit(solution)/shard_map/pallas_call | solution.py:415
  74.2 0.7 copy.18
  74.9 0.7 copy.19
  75.6 0.7 copy.20
  76.3 0.7 copy.21
  77.0 0.6 copy.22
Async XLA Ops:
  0.6 0.7 copy-start.5
  1.3 0.9 %copy-start = (bf16[256,512]{1,0:T(8,128)(2,1)S(1)}, bf16[256,512]{1,0:T(8,128)(2,1)}, u32[]{:S(2)}) copy-start(bf16[256,512]{1,0:T(8,128)(2,1)} %q_hbm.1) | copy-start | bytes 786436
  2.3 0.9 %copy-start.1 = (bf16[256,512]{1,0:T(8,128)(2,1)S(1)}, bf16[256,512]{1,0:T(8,128)(2,1)}, u32[]{:S(2)}) copy-start(bf16[256,512]{1,0:T(8,128)(2,1)} %k_hbm.1) | copy-start | bytes 786436
  3.2 0.9 %copy-start.2 = (bf16[256,512]{1,0:T(8,128)(2,1)S(1)}, bf16[256,512]{1,0:T(8,128)(2,1)}, u32[]{:S(2)}) copy-start(bf16[256,512]{1,0:T(8,128)(2,1)} %v_hbm.1) | copy-start | bytes 786436
  4.2 0.9 %copy-start.3 = (bf16[256,512]{1,0:T(8,128)(2,1)S(1)}, bf16[256,512]{1,0:T(8,128)(2,1)}, u32[]{:S(2)}) copy-start(bf16[256,512]{1,0:T(8,128)(2,1)} %y_hbm.1) | copy-start | bytes 786436
  5.1 0.7 copy-start.4

commit v2 on v1

v2 whole, which is shorter than its diff:
```python
import jax
import jax.numpy as jnp
from jax import lax
from jax.experimental import pallas as pl
from jax.experimental.pallas import tpu as pltpu
from jax.sharding import PartitionSpec as P

HEADS = 32
HEAD_DIM = 128
D = HEADS * HEAD_DIM
EPSILON = 1e-06
ROWS = 256
LOCAL = 4
WIDE = LOCAL * HEAD_DIM
SIDE = 4
CUBE = 16
GROUPS = 4
PIECE = 32
PARTS = 2
SLAB = PIECE // PARTS
HEAD_PEERS = 8
MAIN_VMEM = 40 * 1024 * 1024
LAST_VMEM = 8 * 1024 * 1024
MESH = pl.DeviceIdType.MESH
F32 = jnp.float32
BF16 = jnp.bfloat16
OFFSETS = [(dz, dy) for dz in (2, 1, 3, 0) for dy in (2, 1, 3, 0) if (dz, dy) != (0, 0)]


def dot(a, b, ca, cb):
    return lax.dot_general(a, b, (((ca,), (cb,)), ((), ())), preferred_element_type=F32)


def halves(x):
    upper = x.astype(BF16)
    return upper, (x - upper.astype(F32)).astype(BF16)


def cols(h):
    return pl.ds(h * HEAD_DIM, HEAD_DIM)


def slab(part):
    return pl.ds(part * SLAB, SLAB)


def remote(src, dst, send, recv, where):
    return pltpu.make_async_remote_copy(
        src_ref=src, dst_ref=dst, send_sem=send, recv_sem=recv, device_id=where, device_id_type=MESH
    )


def main_kernel(
    q_hbm, k_hbm, v_hbm, y_hbm, gain_hbm, live_ref, doc_hbm,
    normed_ref, dq_ref, dkl_ref, dvl_ref, kt_ref, vt_ref, r_ref, dgain_ref,
    q_ref, k_ref, v_ref, y_ref, gain_ref, doc_ref,
    mask_ref, w_ref, att_ref, ga_ref, qh_ref, qht_ref,
    flag_src, flag_buf, keep_buf,
    t_ref, tin_ref, pre_ref, tot_ref, totin_ref, carry_ref, sout_ref, s_ref,
    h_ref, hin_ref, htot_ref, htotin_ref, rout_ref,
    ps_src, ps_buf, gg_src, gg_buf, gt_src, gt_buf,
    in_sem, ready, f_sem, ps_sem, gg_sem, gt_sem,
    l1s, l1r, l2s, l2r, l3s, l3r, b1s, b1r, b2s, b2r, b3s, b3r,
):
    c = lax.axis_index("ctx")
    me = lax.axis_index("head")
    p = lax.rem(c, CUBE)
    g = lax.div(c, CUBE)
    base = g * CUBE
    zl = lax.div(p, SIDE)
    yl = lax.rem(p, SIDE)
    ranks = [lax.rem(zl + dz, SIDE) * SIDE + lax.rem(yl + dy, SIDE) for dz, dy in OFFSETS]

    loads = [
        pltpu.make_async_copy(src, dst, in_sem.at[i])
        for i, (src, dst) in enumerate(
            (
                (k_hbm, k_ref), (v_hbm, v_ref), (doc_hbm, doc_ref),
                (q_hbm, q_ref), (y_hbm, y_ref), (gain_hbm, gain_ref),
            )
        )
    ]
    for load in loads:
        load.start()

    def above(b):
        return {"ctx": lax.rem(g + b, GROUPS) * CUBE + p}

    def below(b):
        return {"ctx": lax.rem(g + GROUPS - b, GROUPS) * CUBE + p}

    barrier = pltpu.get_barrier_semaphore()
    for b in range(1, GROUPS):
        @pl.when(g + b < GROUPS)
        def _():
            pl.semaphore_signal(barrier, inc=1, device_id=above(b), device_id_type=MESH)

    for i in ranks:
        pl.semaphore_signal(barrier, inc=1, device_id={"ctx": base + i}, device_id_type=MESH)
    for a in range(1, HEAD_PEERS):
        pl.semaphore_signal(
            barrier, inc=1, device_id={"head": lax.rem(me + a, HEAD_PEERS)}, device_id_type=MESH
        )

    loads[2].wait()
    live = live_ref[0]
    lane = lax.broadcasted_iota(jnp.int32, (ROWS, ROWS), 1)
    sub = lax.broadcasted_iota(jnp.int32, (ROWS, ROWS), 0)
    row8 = lax.broadcasted_iota(jnp.int32, (8, ROWS), 1)
    docs = jnp.broadcast_to(doc_ref[...].reshape(1, ROWS), (8, ROWS))
    starts = jnp.where(row8 < live, docs, 0).astype(F32).astype(BF16)
    upto = jnp.where(sub <= lane, 1.0, 0.0).astype(BF16)
    since = jnp.where(lane <= sub, 1.0, 0.0).astype(BF16)
    id_row = dot(starts, upto, 1, 0)[0:1, :]
    id_col = dot(since, starts, 1, 1)[:, 0:1]
    last = id_row[:, ROWS - 1 : ROWS]
    col = lax.broadcasted_iota(jnp.int32, (ROWS, 1), 0)
    live_col = jnp.where(col < live, 1.0, 0.0)
    tail_col = jnp.where(id_col == last, live_col, 0.0)
    head_col = jnp.where(id_col == 0.0, live_col, 0.0)
    flag = jnp.broadcast_to(jnp.where(last > 0.0, 1.0, 0.0), (1, HEAD_DIM))
    flag_src[...] = flag
    flag_buf[p] = flag
    tail_b = jnp.broadcast_to(tail_col, (ROWS, HEAD_DIM)).astype(BF16)
    head_b = jnp.broadcast_to(head_col, (ROWS, HEAD_DIM)).astype(BF16)
    live_b = jnp.broadcast_to(live_col, (ROWS, HEAD_DIM))

    loads[0].wait()
    loads[1].wait()
    for h in range(LOCAL):
        kt = k_ref[:, cols(h)] * tail_b
        kt_ref[:, cols(h)] = kt
        t_ref[pl.ds(4 * h, 4)] = dot(kt, v_ref[:, cols(h)], 0, 0).reshape(4, PIECE, HEAD_DIM)
    tin_ref[p] = t_ref[p]

    pl.semaphore_wait(barrier, CUBE - 1 + HEAD_PEERS - 1 + g)
    for b in range(1, GROUPS):
        @pl.when(g - b >= 0)
        def _():
            pl.semaphore_signal(ready.at[b], inc=1, device_id=below(b), device_id_type=MESH)

    flags = [remote(flag_src, flag_buf.at[p], f_sem.at[0], f_sem.at[1], {"ctx": base + i}) for i in ranks]
    for copy in flags:
        copy.start()

    def spread(src, dst, send, recv, part):
        for i in ranks:
            remote(
                src.at[i, slab(part)], dst.at[p, slab(part)], send.at[part], recv.at[part], {"ctx": base + i}
            ).start()

    def spread_all(ref, send, recv, part):
        whole = ref.at[pl.ds(0, CUBE - 1), slab(part)]
        return remote(whole, whole, send.at[part], recv.at[part], {"ctx": base + ranks[0]})

    def many(ref, count, sem, where):
        whole = ref.at[pl.ds(0, count)]
        return remote(whole, whole, sem.at[0], sem.at[1], where)

    near = {"ctx": base + ranks[0]}
    for part in range(PARTS):
        spread(t_ref, tin_ref, l1s, l1r, part)

    mask_ref[...] = jnp.where((id_col == id_row) & (lane <= sub), live_col, 0.0)
    loads[3].wait()
    for h in range(LOCAL):
        qs = q_ref[:, cols(h)]
        scores = dot(qs, k_ref[:, cols(h)], 1, 1)
        weights = (scores * mask_ref[...]).astype(BF16)
        w_ref[h] = weights
        att_ref[:, cols(h)] = dot(weights, v_ref[:, cols(h)], 1, 0)
        qh = qs * head_b
        qh_ref[:, cols(h)] = qh
        qht_ref[h] = qh.T
        vt_ref[:, cols(h)] = v_ref[:, cols(h)] * tail_b
    loads[4].wait()
    loads[5].wait()

    many(flag_buf, CUBE - 1, f_sem, near).wait_recv()
    keep = jnp.ones((1, HEAD_DIM), F32)
    for i in range(CUBE):
        keep_buf[i] = keep
        keep = keep * (1.0 - flag_buf[i])
    flag_tile = jnp.broadcast_to(1.0 - keep, (8, HEAD_DIM))
    tot_ref[pl.ds(0, 8)] = flag_tile
    htot_ref[pl.ds(0, 8)] = flag_tile

    def span(part):
        return pl.ds(0, 8 + SLAB) if part == 0 else pl.ds(8 + SLAB, SLAB)

    def rows_of(part):
        return pl.ds(8 + part * SLAB, SLAB)

    def up(b, part):
        return remote(
            tot_ref.at[span(part)], totin_ref.at[g, span(part)], l2s.at[part, b], l2r.at[part, b], above(b)
        )

    def down(b, part):
        return remote(
            htot_ref.at[span(part)], htotin_ref.at[g, span(part)], b2s.at[part, b], b2r.at[part, b], below(b)
        )

    def fold(order, source, partial, total, part):
        acc = jnp.zeros((SLAB, HEAD_DIM), F32)
        for i in order:
            partial[i, slab(part)] = acc
            acc = source[i, slab(part)] + (1.0 - flag_buf[i]) * acc
        total[rows_of(part)] = acc

    def finish(partial, out, into, send, recv, part):
        carry = carry_ref[slab(part)]
        for i in ranks:
            out[i, slab(part)] = partial[i, slab(part)] + keep_buf[i] * carry
            remote(
                out.at[i, slab(part)], into.at[p, slab(part)], send.at[part], recv.at[part], {"ctx": base + i}
            ).start()
        into[p, slab(part)] = partial[p, slab(part)] + keep_buf[p] * carry

    for part in range(PARTS):
        spread_all(tin_ref, l1s, l1r, part).wait_recv()
        fold(range(CUBE), tin_ref, pre_ref, tot_ref, part)
        for b in range(1, GROUPS):
            @pl.when(g + b < GROUPS)
            def _():
                if part == 0:
                    pl.semaphore_wait(ready.at[b], 1)
                up(b, part).start()

    for part in range(PARTS):
        carry_ref[slab(part)] = jnp.zeros((SLAB, HEAD_DIM), F32)
        for b in range(GROUPS - 1, 0, -1):
            @pl.when(g - b >= 0)
            def _():
                up(b, part).wait_recv()
                at = lax.rem(g + GROUPS - b, GROUPS)
                hold = 1.0 - totin_ref[at, pl.ds(0, 1), :]
                carry_ref[slab(part)] = totin_ref[at, rows_of(part), :] + hold * carry_ref[slab(part)]

        finish(pre_ref, sout_ref, s_ref, l3s, l3r, part)
    for part in range(PARTS):
        spread_all(s_ref, l3s, l3r, part).wait_recv()

    square = jnp.zeros((ROWS, HEAD_DIM), F32)
    inner = jnp.zeros((ROWS, HEAD_DIM), F32)
    for h in range(LOCAL):
        upper, lower = halves(s_ref[pl.ds(4 * h, 4)].reshape(HEAD_DIM, HEAD_DIM))
        qh = qh_ref[:, cols(h)]
        att = att_ref[:, cols(h)] + dot(
            jnp.concatenate([qh, qh], axis=1), jnp.concatenate([upper, lower], axis=0), 1, 0
        )
        att_ref[:, cols(h)] = att
        square = square + att * att
        gains = gain_ref[cols(h)].reshape(1, HEAD_DIM)
        inner = inner + att * (y_ref[:, cols(h)].astype(F32) * gains)
    ones = jnp.ones((8, 2 * HEAD_DIM), BF16)
    sums = [dot(ones, jnp.concatenate(halves(x), axis=1), 1, 1)[0:1, :] for x in (square, inner)]
    sums = jnp.concatenate(sums, axis=1)
    ps_src[...] = sums
    ps_buf[me] = sums
    for a in range(1, HEAD_PEERS):
        remote(
            ps_src, ps_buf.at[me], ps_sem.at[0], ps_sem.at[1], {"head": lax.rem(me + a, HEAD_PEERS)}
        ).start()
    side = {"head": lax.rem(me + 1, HEAD_PEERS)}
    many(ps_buf, HEAD_PEERS - 1, ps_sem, side).wait_recv()
    sums = ps_buf[0]
    for i in range(1, HEAD_PEERS):
        sums = sums + ps_buf[i]
    inverse = lax.rsqrt(sums[:, :ROWS] / D + EPSILON)
    factor = sums[:, ROWS:] * (inverse * inverse * inverse / D)
    inverse_col = jnp.broadcast_to(inverse, (HEAD_DIM, ROWS)).T
    factor_col = jnp.broadcast_to(factor, (HEAD_DIM, ROWS)).T

    for h in range(LOCAL):
        att = att_ref[:, cols(h)]
        y = y_ref[:, cols(h)].astype(F32)
        gains = gain_ref[cols(h)].reshape(1, HEAD_DIM)
        ga = ((y * gains) * inverse_col - att * factor_col) * live_b
        ga = ga.astype(BF16)
        ga_ref[:, cols(h)] = ga
        h_ref[pl.ds(4 * h, 4)] = dot(qht_ref[h], ga, 1, 0).reshape(4, PIECE, HEAD_DIM)
    hin_ref[p] = h_ref[p]
    for part in range(PARTS):
        spread(h_ref, hin_ref, b1s, b1r, part)

    gain_terms = []
    for h in range(LOCAL):
        att = att_ref[:, cols(h)]
        y = y_ref[:, cols(h)].astype(F32)
        gains = gain_ref[cols(h)].reshape(1, HEAD_DIM)
        unit = att * inverse_col
        normed_ref[:, cols(h)] = (unit * gains).astype(BF16)
        gain_terms.append(jnp.sum(y * unit, axis=0, keepdims=True))
    gain_term = jnp.concatenate(gain_terms, axis=1)
    gg_src[...] = gain_term
    gg_buf[p] = gain_term
    for i in ranks:
        remote(gg_src, gg_buf.at[p], gg_sem.at[0], gg_sem.at[1], {"ctx": base + i}).start()
    for h in range(LOCAL):
        ga = ga_ref[:, cols(h)]
        probes = (dot(ga, v_ref[:, cols(h)], 1, 1) * mask_ref[...]).astype(BF16)
        upper, lower = halves(s_ref[pl.ds(4 * h, 4)].reshape(HEAD_DIM, HEAD_DIM))
        gh = ga * head_b
        carried = dot(jnp.concatenate([gh, gh], axis=1), jnp.concatenate([upper, lower], axis=1), 1, 1)
        dq_ref[:, cols(h)] = (dot(probes, k_ref[:, cols(h)], 1, 0) + carried).astype(BF16)
        dkl_ref[:, cols(h)] = dot(probes, q_ref[:, cols(h)], 0, 0)
    keep = jnp.ones((1, HEAD_DIM), F32)
    for i in range(CUBE - 1, -1, -1):
        keep_buf[i] = keep
        keep = keep * (1.0 - flag_buf[i])

    for part in range(PARTS):
        spread_all(hin_ref, b1s, b1r, part).wait_recv()
        fold(range(CUBE - 1, -1, -1), hin_ref, pre_ref, htot_ref, part)
        for b in range(1, GROUPS):
            @pl.when(g - b >= 0)
            def _():
                down(b, part).start()

    many(gg_buf, CUBE - 1, gg_sem, near).wait_recv()
    total = gg_buf[0]
    for i in range(1, CUBE):
        total = total + gg_buf[i]
    gt_src[...] = total
    gt_buf[g] = total
    for b in range(1, GROUPS):
        remote(gt_src, gt_buf.at[g], gt_sem.at[0], gt_sem.at[1], above(b)).start()

    for h in range(LOCAL):
        dvl_ref[:, cols(h)] = dot(w_ref[h], ga_ref[:, cols(h)], 0, 0)

    for part in range(PARTS):
        carry_ref[slab(part)] = jnp.zeros((SLAB, HEAD_DIM), F32)
        for b in range(GROUPS - 1, 0, -1):
            @pl.when(g + b < GROUPS)
            def _():
                down(b, part).wait_recv()
                at = lax.rem(g + b, GROUPS)
                hold = 1.0 - htotin_ref[at, pl.ds(0, 1), :]
                carry_ref[slab(part)] = htotin_ref[at, rows_of(part), :] + hold * carry_ref[slab(part)]

        finish(pre_ref, rout_ref, r_ref, b3s, b3r, part)

    many(gt_buf, GROUPS - 1, gt_sem, above(1)).wait_recv()
    dgain_ref[...] = (((gt_buf[0] + gt_buf[1]) + gt_buf[2]) + gt_buf[3]).reshape(WIDE)

    many(flag_buf, CUBE - 1, f_sem, near).wait_send()
    many(ps_buf, HEAD_PEERS - 1, ps_sem, side).wait_send()
    many(gg_buf, CUBE - 1, gg_sem, near).wait_send()
    many(gt_buf, GROUPS - 1, gt_sem, above(1)).wait_send()
    for part in range(PARTS):
        spread_all(t_ref, l1s, l1r, part).wait_send()
        spread_all(sout_ref, l3s, l3r, part).wait_send()
        spread_all(h_ref, b1s, b1r, part).wait_send()
        for b in range(1, GROUPS):
            @pl.when(g + b < GROUPS)
            def _():
                up(b, part).wait_send()

            @pl.when(g - b >= 0)
            def _():
                down(b, part).wait_send()
    for part in range(PARTS):
        spread_all(rout_ref, b3s, b3r, part).wait_send()
    for part in range(PARTS):
        spread_all(r_ref, b3s, b3r, part).wait_recv()


def last_kernel(
    normed_ref, dq_ref, dkl_ref, dvl_ref, kt_ref, vt_ref, r_ref, dgain_ref,
    normed_hbm, dq_hbm, dk_hbm, dv_hbm, dgain_hbm,
    dk_ref, dv_ref, sems,
):
    stores = [
        pltpu.make_async_copy(src, dst, sems.at[i])
        for i, (src, dst) in enumerate(
            ((normed_ref, normed_hbm), (dq_ref, dq_hbm), (dgain_ref, dgain_hbm))
        )
    ]
    for store in stores:
        store.start()
    for h in range(LOCAL):
        upper, lower = halves(r_ref[pl.ds(4 * h, 4)].reshape(HEAD_DIM, HEAD_DIM))
        vt = vt_ref[:, cols(h)]
        kt = kt_ref[:, cols(h)]
        dk = dkl_ref[:, cols(h)] + dot(
            jnp.concatenate([vt, vt], axis=1), jnp.concatenate([upper, lower], axis=1), 1, 1
        )
        dk_ref[:, cols(h)] = dk.astype(BF16)
        dv = dvl_ref[:, cols(h)] + dot(
            jnp.concatenate([kt, kt], axis=1), jnp.concatenate([upper, lower], axis=0), 1, 0
        )
        dv_ref[:, cols(h)] = dv.astype(BF16)
        for i, (src, dst) in enumerate(((dk_ref, dk_hbm), (dv_ref, dv_hbm))):
            store = pltpu.make_async_copy(src.at[:, cols(h)], dst.at[:, cols(h)], sems.at[3 + 2 * h + i])
            store.start()
            stores.append(store)
    for store in stores:
        store.wait()


def stay(x):
    return pltpu.with_memory_space_constraint(x, pltpu.HBM)


def per_device(queries, keys, values, d_out, gain, live_rows, doc_start):
    hbm = pl.BlockSpec(memory_space=pltpu.HBM)
    vmem = pl.BlockSpec(memory_space=pltpu.VMEM)
    block = (ROWS, WIDE)
    pieces = (CUBE, PIECE, HEAD_DIM)
    total = (PIECE + 8, HEAD_DIM)
    dma = pltpu.SemaphoreType.DMA
    scratch = [pltpu.VMEM(block, BF16)] * 4
    scratch += [pltpu.VMEM((WIDE,), F32), pltpu.VMEM((ROWS,), jnp.int32)]
    scratch += [
        pltpu.VMEM((ROWS, ROWS), F32),
        pltpu.VMEM((LOCAL, ROWS, ROWS), BF16),
        pltpu.VMEM(block, F32),
        pltpu.VMEM(block, BF16),
        pltpu.VMEM(block, BF16),
        pltpu.VMEM((LOCAL, HEAD_DIM, ROWS), BF16),
    ]
    scratch += [
        pltpu.VMEM((1, HEAD_DIM), F32),
        pltpu.VMEM((CUBE, 1, HEAD_DIM), F32),
        pltpu.VMEM((CUBE, 1, HEAD_DIM), F32),
    ]
    scratch += [pltpu.VMEM(pieces, F32)] * 3
    scratch += [
        pltpu.VMEM(total, F32),
        pltpu.VMEM((GROUPS,) + total, F32),
        pltpu.VMEM((PIECE, HEAD_DIM), F32),
    ]
    scratch += [pltpu.VMEM(pieces, F32)] * 4
    scratch += [pltpu.VMEM(total, F32), pltpu.VMEM((GROUPS,) + total, F32), pltpu.VMEM(pieces, F32)]
    scratch += [
        pltpu.VMEM((1, 2 * ROWS), F32),
        pltpu.VMEM((HEAD_PEERS, 1, 2 * ROWS), F32),
        pltpu.VMEM((1, WIDE), F32),
        pltpu.VMEM((CUBE, 1, WIDE), F32),
        pltpu.VMEM((1, WIDE), F32),
        pltpu.VMEM((GROUPS, 1, WIDE), F32),
    ]
    scratch += [dma((6,)), pltpu.SemaphoreType.REGULAR((GROUPS,))] + [dma((2,))] * 4
    one, pairs = dma((PARTS,)), dma((PARTS, GROUPS))
    scratch += [one, one, pairs, pairs, one, one] * 2
    shape = jax.ShapeDtypeStruct(block, BF16)
    wide = jax.ShapeDtypeStruct(block, F32)
    gains = jax.ShapeDtypeStruct((WIDE,), F32)
    made = pl.pallas_call(
        main_kernel,
        out_shape=(shape, shape, wide, wide, shape, shape, jax.ShapeDtypeStruct(pieces, F32), gains),
        in_specs=[hbm] * 5 + [pl.BlockSpec(memory_space=pltpu.SMEM), hbm],
        out_specs=(vmem,) * 8,
        scratch_shapes=scratch,
        compiler_params=pltpu.CompilerParams(
            collective_id=0, has_side_effects=True, vmem_limit_bytes=MAIN_VMEM
        ),
    )(*(stay(x) for x in (queries, keys, values, d_out, gain)), live_rows, stay(doc_start))
    return pl.pallas_call(
        last_kernel,
        out_shape=(shape, shape, shape, shape, gains),
        in_specs=[vmem] * 8,
        out_specs=(hbm,) * 5,
        scratch_shapes=[pltpu.VMEM(block, BF16)] * 2 + [dma((3 + 2 * LOCAL,))],
        compiler_params=pltpu.CompilerParams(vmem_limit_bytes=LAST_VMEM),
    )(*made)


def solution(mesh):
    block = P("ctx", "head")
    return jax.shard_map(
        per_device,
        mesh=mesh,
        in_specs=(block, block, block, block, P("head"), P("ctx"), P("ctx")),
        out_specs=(block, block, block, block, P("head")),
        check_vma=False,
    )
```

time: 78.3 us -> 62.9 us (0.80)
  the two profiles are of different devices: /device:TPU:1 before, /device:TPU:2 now
where the time goes in v2:
time: 62.9 us; the launch traced here: 62.8 us
  Pallas kernels  61.5 us (98%)
  between operations  1.29 us (2%)
    pallas_call x1, Pallas kernels, per_device(): pl.pallas_call(main_kernel, out_shape=(shape, shape, wide, wide, shape, s...  60.3 us

profile of v2, /device:TPU:2, one launch (start us, length us, event | category | flops | bytes accessed | tf_op | source)
XLA Modules:
  0.0 62.8 jit_solution(4920381325799773455)
XLA Ops:
  1.3 60.3 %shard_map.110 = (bf16[256,512]{1,0:T(8,128)(2,1)S(1)}, bf16[256,512]{1,0:T(8,128)(2,1)S(1)}, f32[256,512]{1,0:T(8,128)S(1)}, f32[256,512]{1,0:T(8,128)S(1)}, bf...) custom-call(bf16[256,512]{1,0:T(8,128)(2,1)} %q_hbm.1, ...), custom_call_target="tpu_custom_call" | custom-call | tf_op jit(solution)/shard_map/pallas_call | solution.py:451
  61.6 1.2 %shard_map.111 = (bf16[256,512]{1,0:T(8,128)(2,1)}, bf16[256,512]{1,0:T(8,128)(2,1)}, bf16[256,512]{1,0:T(8,128)(2,1)}, bf16[256,512]{1,0:T(8,128)(2,1)}, f32[512]{0:T(512)}) custom-call(bf16[256,512]{1,0:T(8,128)(2,1)S(1)} %get-tuple-element.13.normed_ref, bf16[256,512]{1,0:T(8,128)(2,1)S(1)} %get-tuple-element.14.dq_ref, ...), custom_call_target="tpu_custom_call" | custom-call | tf_op jit(solution)/shard_map/pallas_call | solution.py:461

commit v3 on v2

v3 whole, which is shorter than its diff:
```python
import jax
import jax.numpy as jnp
from jax import lax
from jax.experimental import pallas as pl
from jax.experimental.pallas import tpu as pltpu
from jax.sharding import PartitionSpec as P

HEADS = 32
HEAD_DIM = 128
D = HEADS * HEAD_DIM
EPSILON = 1e-06
ROWS = 256
LOCAL = 4
WIDE = LOCAL * HEAD_DIM
SIDE = 4
CUBE = 16
GROUPS = 4
PARTS = 4
PER = LOCAL // PARTS
SHARE = CUBE // PER
SLAB = 8 * PER
HEAD_PEERS = 8
MAIN_VMEM = 40 * 1024 * 1024
LAST_VMEM = 8 * 1024 * 1024
MESH = pl.DeviceIdType.MESH
F32 = jnp.float32
BF16 = jnp.bfloat16
OFFSETS = [(dz, dy) for dz in (2, 1, 3, 0) for dy in (2, 1, 3, 0) if (dz, dy) != (0, 0)]


def dot(a, b, ca, cb):
    return lax.dot_general(a, b, (((ca,), (cb,)), ((), ())), preferred_element_type=F32)


def halves(x):
    upper = x.astype(BF16)
    return upper, (x - upper.astype(F32)).astype(BF16)


def cols(h):
    return pl.ds(h * HEAD_DIM, HEAD_DIM)


def part_of(h):
    return h // PER


def share(h):
    return pl.ds(h % PER * SHARE, SHARE)


def remote(src, dst, send, recv, where):
    return pltpu.make_async_remote_copy(
        src_ref=src, dst_ref=dst, send_sem=send, recv_sem=recv, device_id=where, device_id_type=MESH
    )


def main_kernel(
    q_hbm, k_hbm, v_hbm, y_hbm, gain_hbm, live_ref, doc_hbm,
    normed_ref, dq_ref, dk_ref, dv_ref, dgain_ref,
    q_ref, k_ref, v_ref, y_ref, gain_ref, doc_ref,
    mask_ref, w_ref, att_ref, scaled_ref, dkl_ref, dvl_ref, ga_ref, qh_ref, kt_ref, vt_ref, qht_ref,
    flag_src, flag_buf, keep_buf,
    t_ref, tin_ref, pre_ref, tot_ref, totin_ref, carry_ref, sout_ref, s_ref,
    h_ref, hin_ref, htot_ref, htotin_ref, rout_ref, r_ref,
    ps_src, ps_buf, gy_src, gy_buf, gg_src, gg_buf, gt_src, gt_buf,
    in_sem, ready, f_sem, ps_sem, gy_sem, gg_sem, gt_sem,
    l1s, l1r, l2s, l2r, l3s, l3r, b1s, b1r, b2s, b2r, b3s, b3r,
):
    c = lax.axis_index("ctx")
    me = lax.axis_index("head")
    p = lax.rem(c, CUBE)
    g = lax.div(c, CUBE)
    base = g * CUBE
    zl = lax.div(p, SIDE)
    yl = lax.rem(p, SIDE)
    ranks = [lax.rem(zl + dz, SIDE) * SIDE + lax.rem(yl + dy, SIDE) for dz, dy in OFFSETS]

    loads = [
        pltpu.make_async_copy(src, dst, in_sem.at[i])
        for i, (src, dst) in enumerate(
            (
                (k_hbm, k_ref), (v_hbm, v_ref), (doc_hbm, doc_ref),
                (q_hbm, q_ref), (y_hbm, y_ref), (gain_hbm, gain_ref),
            )
        )
    ]
    for load in loads:
        load.start()

    def above(b):
        return {"ctx": lax.rem(g + b, GROUPS) * CUBE + p}

    def below(b):
        return {"ctx": lax.rem(g + GROUPS - b, GROUPS) * CUBE + p}

    def along_y(a):
        return {"ctx": base + zl * SIDE + lax.rem(yl + a, SIDE)}

    def along_z(a):
        return {"ctx": base + lax.rem(zl + a, SIDE) * SIDE + yl}

    barrier = pltpu.get_barrier_semaphore()
    for b in range(1, GROUPS):
        @pl.when(g + b < GROUPS)
        def _():
            pl.semaphore_signal(barrier, inc=1, device_id=above(b), device_id_type=MESH)

    for i in ranks:
        pl.semaphore_signal(barrier, inc=1, device_id={"ctx": base + i}, device_id_type=MESH)
    for a in range(1, HEAD_PEERS):
        pl.semaphore_signal(
            barrier, inc=1, device_id={"head": lax.rem(me + a, HEAD_PEERS)}, device_id_type=MESH
        )

    loads[2].wait()
    live = live_ref[0]
    lane1 = lax.broadcasted_iota(jnp.int32, (1, ROWS), 1)
    starts = (doc_ref[...].reshape(1, ROWS) > 0) & (lane1 < live)
    place = lane1.astype(F32)
    final = jnp.max(jnp.where(starts, place, -1.0), axis=1, keepdims=True)
    first = jnp.min(jnp.where(starts, place, float(ROWS)), axis=1, keepdims=True)
    col = lax.broadcasted_iota(jnp.int32, (ROWS, HEAD_DIM), 0)
    live_b = jnp.where(col < live, 1.0, 0.0)
    place_b = col.astype(F32)
    tail_b = jnp.where(place_b >= final, live_b, 0.0).astype(BF16)
    head_b = jnp.where(place_b < first, live_b, 0.0).astype(BF16)
    flag = jnp.broadcast_to(jnp.where(final >= 0.0, 1.0, 0.0), (1, HEAD_DIM))
    flag_src[...] = flag
    flag_buf[p] = flag

    loads[0].wait()
    loads[1].wait()
    for h in range(LOCAL):
        kt = k_ref[:, cols(h)] * tail_b
        kt_ref[:, cols(h)] = kt
        t_ref[part_of(h), share(h)] = dot(kt, v_ref[:, cols(h)], 0, 0).reshape(SHARE, SLAB, HEAD_DIM)
    for s in range(PARTS):
        tin_ref[s, p] = t_ref[s, p]

    pl.semaphore_wait(barrier, CUBE - 1 + HEAD_PEERS - 1 + g)
    for b in range(1, GROUPS):
        @pl.when(g - b >= 0)
        def _():
            pl.semaphore_signal(ready.at[b], inc=1, device_id=below(b), device_id_type=MESH)

    flags = [remote(flag_src, flag_buf.at[p], f_sem.at[0], f_sem.at[1], {"ctx": base + i}) for i in ranks]
    for copy in flags:
        copy.start()

    def spread(src, dst, send, recv, h):
        for i in ranks:
            remote(src.at[h, i], dst.at[h, p], send.at[h], recv.at[h], {"ctx": base + i}).start()

    def spread_all(ref, send, recv, h):
        whole = ref.at[h, pl.ds(0, CUBE - 1)]
        return remote(whole, whole, send.at[h], recv.at[h], {"ctx": base + ranks[0]})

    def many(ref, count, sem, where):
        whole = ref.at[pl.ds(0, count)]
        return remote(whole, whole, sem.at[0], sem.at[1], where)

    near = {"ctx": base + ranks[0]}
    for s in range(PARTS):
        spread(t_ref, tin_ref, l1s, l1r, s)

    lane = lax.broadcasted_iota(jnp.int32, (ROWS, ROWS), 1)
    sub = lax.broadcasted_iota(jnp.int32, (ROWS, ROWS), 0)
    upto = jnp.where(sub <= lane, 1.0, 0.0).astype(BF16)
    since = jnp.where(lane <= sub, 1.0, 0.0).astype(BF16)
    starts8 = jnp.broadcast_to(jnp.where(starts, 1.0, 0.0), (8, ROWS)).astype(BF16)
    id_row = dot(starts8, upto, 1, 0)[0:1, :]
    id_col = dot(since, starts8, 1, 1)[:, 0:1]
    live_col = live_b[:, 0:1]
    mask_ref[...] = jnp.where((id_col == id_row) & (lane <= sub), live_col, 0.0)
    loads[3].wait()
    for h in range(LOCAL):
        qs = q_ref[:, cols(h)]
        scores = dot(qs, k_ref[:, cols(h)], 1, 1)
        weights = (scores * mask_ref[...]).astype(BF16)
        w_ref[h] = weights
        att_ref[:, cols(h)] = dot(weights, v_ref[:, cols(h)], 1, 0)
        qh = qs * head_b
        qh_ref[:, cols(h)] = qh
        qht_ref[h] = qh.T
        vt_ref[:, cols(h)] = v_ref[:, cols(h)] * tail_b
    loads[4].wait()
    loads[5].wait()
    for h in range(LOCAL):
        scaled_ref[:, cols(h)] = y_ref[:, cols(h)].astype(F32) * gain_ref[cols(h)].reshape(1, HEAD_DIM)

    many(flag_buf, CUBE - 1, f_sem, near).wait_recv()
    keep = jnp.ones((1, HEAD_DIM), F32)
    for i in range(CUBE):
        keep_buf[i] = keep
        keep = keep * (1.0 - flag_buf[i])
    flag_tile = jnp.broadcast_to(1.0 - keep, (8, HEAD_DIM))
    tot_ref[pl.ds(0, 8)] = flag_tile
    htot_ref[pl.ds(0, 8)] = flag_tile

    def span(s):
        return pl.ds(0, 8 + SLAB) if s == 0 else rows_of(s)

    def rows_of(s):
        return pl.ds(8 + s * SLAB, SLAB)

    def up(b, s):
        return remote(tot_ref.at[span(s)], totin_ref.at[g, span(s)], l2s.at[s, b], l2r.at[s, b], above(b))

    def down(b, s):
        return remote(htot_ref.at[span(s)], htotin_ref.at[g, span(s)], b2s.at[s, b], b2r.at[s, b], below(b))

    def fold(order, source, partial, total, s):
        acc = jnp.zeros((SLAB, HEAD_DIM), F32)
        for i in order:
            partial[s, i] = acc
            acc = source[s, i] + (1.0 - flag_buf[i]) * acc
        total[rows_of(s)] = acc

    def finish(partial, out, into, send, recv, s):
        carry = carry_ref[s]
        for i in ranks:
            out[s, i] = partial[s, i] + keep_buf[i] * carry
            remote(out.at[s, i], into.at[s, p], send.at[s], recv.at[s], {"ctx": base + i}).start()
        into[s, p] = partial[s, p] + keep_buf[p] * carry

    for s in range(PARTS):
        spread_all(tin_ref, l1s, l1r, s).wait_recv()
        fold(range(CUBE), tin_ref, pre_ref, tot_ref, s)
        for b in range(1, GROUPS):
            @pl.when(g + b < GROUPS)
            def _():
                if s == 0:
                    pl.semaphore_wait(ready.at[b], 1)
                up(b, s).start()

    for s in range(PARTS):
        carry_ref[s] = jnp.zeros((SLAB, HEAD_DIM), F32)
        for b in range(GROUPS - 1, 0, -1):
            @pl.when(g - b >= 0)
            def _():
                up(b, s).wait_recv()
                at = lax.rem(g + GROUPS - b, GROUPS)
                hold = 1.0 - totin_ref[at, pl.ds(0, 1), :]
                carry_ref[s] = totin_ref[at, rows_of(s), :] + hold * carry_ref[s]

        finish(pre_ref, sout_ref, s_ref, l3s, l3r, s)

    square = jnp.zeros((ROWS, HEAD_DIM), F32)
    inner = jnp.zeros((ROWS, HEAD_DIM), F32)
    for h in range(LOCAL):
        if h % PER == 0:
            spread_all(s_ref, l3s, l3r, part_of(h)).wait_recv()
        upper, lower = halves(s_ref[part_of(h), share(h)].reshape(HEAD_DIM, HEAD_DIM))
        qh = qh_ref[:, cols(h)]
        att = att_ref[:, cols(h)] + dot(
            jnp.concatenate([qh, qh], axis=1), jnp.concatenate([upper, lower], axis=0), 1, 0
        )
        att_ref[:, cols(h)] = att
        square = square + att * att
        inner = inner + att * scaled_ref[:, cols(h)]
    ones = jnp.ones((8, 2 * HEAD_DIM), BF16)
    sums = [dot(ones, jnp.concatenate(halves(x), axis=1), 1, 1)[0:1, :] for x in (square, inner)]
    sums = jnp.concatenate(sums, axis=1)
    ps_src[...] = sums
    ps_buf[me] = sums
    for a in range(1, HEAD_PEERS):
        remote(
            ps_src, ps_buf.at[me], ps_sem.at[0], ps_sem.at[1], {"head": lax.rem(me + a, HEAD_PEERS)}
        ).start()
    side = {"head": lax.rem(me + 1, HEAD_PEERS)}
    many(ps_buf, HEAD_PEERS - 1, ps_sem, side).wait_recv()
    sums = ps_buf[0]
    for i in range(1, HEAD_PEERS):
        sums = sums + ps_buf[i]
    inverse = lax.rsqrt(sums[:, :ROWS] / D + EPSILON)
    factor = sums[:, ROWS:] * (inverse * inverse * inverse / D)
    alive = jnp.where(lane1 < live, 1.0, 0.0)
    inverse_col = jnp.broadcast_to(inverse * alive, (HEAD_DIM, ROWS)).T
    factor_col = jnp.broadcast_to(factor * alive, (HEAD_DIM, ROWS)).T

    for h in range(LOCAL):
        ga = (scaled_ref[:, cols(h)] * inverse_col - att_ref[:, cols(h)] * factor_col).astype(BF16)
        ga_ref[:, cols(h)] = ga
        h_ref[part_of(h), share(h)] = dot(qht_ref[h], ga, 1, 0).reshape(SHARE, SLAB, HEAD_DIM)
        if h % PER == PER - 1:
            hin_ref[part_of(h), p] = h_ref[part_of(h), p]
            spread(h_ref, hin_ref, b1s, b1r, part_of(h))

    gain_terms = []
    for h in range(LOCAL):
        att = att_ref[:, cols(h)]
        y = y_ref[:, cols(h)].astype(F32)
        gains = gain_ref[cols(h)].reshape(1, HEAD_DIM)
        unit = att * inverse_col
        normed_ref[:, cols(h)] = (unit * gains).astype(BF16)
        gain_terms.append(jnp.sum(y * unit, axis=0, keepdims=True))
    gain_term = jnp.concatenate(gain_terms, axis=1)
    gy_src[...] = gain_term
    gy_buf[yl] = gain_term
    for a in range(1, SIDE):
        remote(gy_src, gy_buf.at[yl], gy_sem.at[0], gy_sem.at[1], along_y(a)).start()
    for h in range(LOCAL):
        ga = ga_ref[:, cols(h)]
        probes = (dot(ga, v_ref[:, cols(h)], 1, 1) * mask_ref[...]).astype(BF16)
        upper, lower = halves(s_ref[part_of(h), share(h)].reshape(HEAD_DIM, HEAD_DIM))
        gh = ga * head_b
        carried = dot(jnp.concatenate([gh, gh], axis=1), jnp.concatenate([upper, lower], axis=1), 1, 1)
        dq_ref[:, cols(h)] = (dot(probes, k_ref[:, cols(h)], 1, 0) + carried).astype(BF16)
        dkl_ref[:, cols(h)] = dot(probes, q_ref[:, cols(h)], 0, 0)
    keep = jnp.ones((1, HEAD_DIM), F32)
    for i in range(CUBE - 1, -1, -1):
        keep_buf[i] = keep
        keep = keep * (1.0 - flag_buf[i])

    many(gy_buf, SIDE - 1, gy_sem, along_y(1)).wait_recv()
    total = ((gy_buf[0] + gy_buf[1]) + gy_buf[2]) + gy_buf[3]
    gg_src[...] = total
    gg_buf[zl] = total
    for a in range(1, SIDE):
        remote(gg_src, gg_buf.at[zl], gg_sem.at[0], gg_sem.at[1], along_z(a)).start()

    for s in range(PARTS):
        spread_all(hin_ref, b1s, b1r, s).wait_recv()
        fold(range(CUBE - 1, -1, -1), hin_ref, pre_ref, htot_ref, s)
        for b in range(1, GROUPS):
            @pl.when(g - b >= 0)
            def _():
                down(b, s).start()

    many(gg_buf, SIDE - 1, gg_sem, along_z(1)).wait_recv()
    total = ((gg_buf[0] + gg_buf[1]) + gg_buf[2]) + gg_buf[3]
    gt_src[...] = total
    gt_buf[g] = total
    for b in range(1, GROUPS):
        remote(gt_src, gt_buf.at[g], gt_sem.at[0], gt_sem.at[1], above(b)).start()

    for h in range(LOCAL):
        dvl_ref[:, cols(h)] = dot(w_ref[h], ga_ref[:, cols(h)], 0, 0)

    for s in range(PARTS):
        carry_ref[s] = jnp.zeros((SLAB, HEAD_DIM), F32)
        for b in range(GROUPS - 1, 0, -1):
            @pl.when(g + b < GROUPS)
            def _():
                down(b, s).wait_recv()
                at = lax.rem(g + b, GROUPS)
                hold = 1.0 - htotin_ref[at, pl.ds(0, 1), :]
                carry_ref[s] = htotin_ref[at, rows_of(s), :] + hold * carry_ref[s]

        finish(pre_ref, rout_ref, r_ref, b3s, b3r, s)

    many(gt_buf, GROUPS - 1, gt_sem, above(1)).wait_recv()
    dgain_ref[...] = (((gt_buf[0] + gt_buf[1]) + gt_buf[2]) + gt_buf[3]).reshape(WIDE)

    many(flag_buf, CUBE - 1, f_sem, near).wait_send()
    many(ps_buf, HEAD_PEERS - 1, ps_sem, side).wait_send()
    many(gy_buf, SIDE - 1, gy_sem, along_y(1)).wait_send()
    many(gg_buf, SIDE - 1, gg_sem, along_z(1)).wait_send()
    many(gt_buf, GROUPS - 1, gt_sem, above(1)).wait_send()
    for s in range(PARTS):
        spread_all(t_ref, l1s, l1r, s).wait_send()
        spread_all(sout_ref, l3s, l3r, s).wait_send()
        spread_all(h_ref, b1s, b1r, s).wait_send()
        for b in range(1, GROUPS):
            @pl.when(g + b < GROUPS)
            def _():
                up(b, s).wait_send()

            @pl.when(g - b >= 0)
            def _():
                down(b, s).wait_send()

    for h in range(LOCAL):
        if h % PER == 0:
            spread_all(r_ref, b3s, b3r, part_of(h)).wait_recv()
        upper, lower = halves(r_ref[part_of(h), share(h)].reshape(HEAD_DIM, HEAD_DIM))
        vt = vt_ref[:, cols(h)]
        kt = kt_ref[:, cols(h)]
        dk = dkl_ref[:, cols(h)] + dot(
            jnp.concatenate([vt, vt], axis=1), jnp.concatenate([upper, lower], axis=1), 1, 1
        )
        dk_ref[:, cols(h)] = dk.astype(BF16)
        dv = dvl_ref[:, cols(h)] + dot(
            jnp.concatenate([kt, kt], axis=1), jnp.concatenate([upper, lower], axis=0), 1, 0
        )
        dv_ref[:, cols(h)] = dv.astype(BF16)
    for s in range(PARTS):
        spread_all(rout_ref, b3s, b3r, s).wait_send()


def last_kernel(*refs):
    sems = refs[10]
    stores = [pltpu.make_async_copy(refs[i], refs[5 + i], sems.at[i]) for i in range(5)]
    for store in stores:
        store.start()
    for store in stores:
        store.wait()


def stay(x):
    return pltpu.with_memory_space_constraint(x, pltpu.HBM)


def per_device(queries, keys, values, d_out, gain, live_rows, doc_start):
    hbm = pl.BlockSpec(memory_space=pltpu.HBM)
    vmem = pl.BlockSpec(memory_space=pltpu.VMEM)
    block = (ROWS, WIDE)
    pieces = (PARTS, CUBE, SLAB, HEAD_DIM)
    total = (8 + PARTS * SLAB, HEAD_DIM)
    dma = pltpu.SemaphoreType.DMA
    scratch = [pltpu.VMEM(block, BF16)] * 4
    scratch += [pltpu.VMEM((WIDE,), F32), pltpu.VMEM((ROWS,), jnp.int32)]
    scratch += [
        pltpu.VMEM((ROWS, ROWS), F32),
        pltpu.VMEM((LOCAL, ROWS, ROWS), BF16),
    ]
    scratch += [pltpu.VMEM(block, F32)] * 4 + [pltpu.VMEM(block, BF16)] * 4
    scratch += [pltpu.VMEM((LOCAL, HEAD_DIM, ROWS), BF16)]
    scratch += [
        pltpu.VMEM((1, HEAD_DIM), F32),
        pltpu.VMEM((CUBE, 1, HEAD_DIM), F32),
        pltpu.VMEM((CUBE, 1, HEAD_DIM), F32),
    ]
    scratch += [pltpu.VMEM(pieces, F32)] * 3
    scratch += [
        pltpu.VMEM(total, F32),
        pltpu.VMEM((GROUPS,) + total, F32),
        pltpu.VMEM((PARTS, SLAB, HEAD_DIM), F32),
    ]
    scratch += [pltpu.VMEM(pieces, F32)] * 4
    scratch += [pltpu.VMEM(total, F32), pltpu.VMEM((GROUPS,) + total, F32)]
    scratch += [pltpu.VMEM(pieces, F32)] * 2
    scratch += [
        pltpu.VMEM((1, 2 * ROWS), F32),
        pltpu.VMEM((HEAD_PEERS, 1, 2 * ROWS), F32),
    ]
    scratch += [pltpu.VMEM((1, WIDE), F32), pltpu.VMEM((GROUPS, 1, WIDE), F32)] * 3
    scratch += [dma((6,)), pltpu.SemaphoreType.REGULAR((GROUPS,))] + [dma((2,))] * 5
    one, pairs = dma((PARTS,)), dma((PARTS, GROUPS))
    scratch += [one, one, pairs, pairs, one, one] * 2
    shape = jax.ShapeDtypeStruct(block, BF16)
    gains = jax.ShapeDtypeStruct((WIDE,), F32)
    made = pl.pallas_call(
        main_kernel,
        out_shape=(shape, shape, shape, shape, gains),
        in_specs=[hbm] * 5 + [pl.BlockSpec(memory_space=pltpu.SMEM), hbm],
        out_specs=(vmem,) * 5,
        scratch_shapes=scratch,
        compiler_params=pltpu.CompilerParams(
            collective_id=0, has_side_effects=True, vmem_limit_bytes=MAIN_VMEM
        ),
    )(*(stay(x) for x in (queries, keys, values, d_out, gain)), live_rows, stay(doc_start))
    return pl.pallas_call(
        last_kernel,
        out_shape=(shape, shape, shape, shape, gains),
        in_specs=[vmem] * 5,
        out_specs=(hbm,) * 5,
        scratch_shapes=[dma((5,))],
        compiler_params=pltpu.CompilerParams(vmem_limit_bytes=LAST_VMEM),
    )(*made)


def solution(mesh):
    block = P("ctx", "head")
    return jax.shard_map(
        per_device,
        mesh=mesh,
        in_specs=(block, block, block, block, P("head"), P("ctx"), P("ctx")),
        out_specs=(block, block, block, block, P("head")),
        check_vma=False,
    )
```

time: 62.9 us -> 61.9 us (0.984)
  the two profiles are of different devices: /device:TPU:2 before, /device:TPU:1 now
where the time goes in v3:
time: 61.9 us; the launch traced here: 60.8 us
  Pallas kernels  59.6 us (96%)
  between operations  1.29 us (2%)
    pallas_call x1, Pallas kernels, per_device(): pl.pallas_call(main_kernel, out_shape=(shape, shape, shape, shape, gains)...  58.5 us

profile of v3, /device:TPU:1, one launch (start us, length us, event | category | flops | bytes accessed | tf_op | source)
XLA Modules:
  0.0 60.8 jit_solution(5444827711319038905)
XLA Ops:
  1.3 58.5 %shard_map.110 = (bf16[256,512]{1,0:T(8,128)(2,1)S(1)}, bf16[256,512]{1,0:T(8,128)(2,1)S(1)}, bf16[256,512]{1,0:T(8,128)(2,1)S(1)}, bf16[256,512]{1,0:T(8,128)(2,1)S(1)}, f32[512]{0:T(512)S(1)}) custom-call(bf16[256,512]{1,0:T(8,128)(2,1)} %q_hbm.1, bf16[256,512]{1,0:T(8,128)(2,1)} %k_hbm.1, bf16[256,512]{1,0:T(8,128)(2,1)} %v_hbm.1, ...), custom_call_target="tpu_custom_call" | custom-call | tf_op jit(solution)/shard_map/pallas_call | solution.py:444
  59.8 1.0 %shard_map.111 = (bf16[256,512]{1,0:T(8,128)(2,1)}, bf16[256,512]{1,0:T(8,128)(2,1)}, bf16[256,512]{1,0:T(8,128)(2,1)}, bf16[256,512]{1,0:T(8,128)(2,1)}, f32[512]{0:T(512)}) custom-call(bf16[256,512]{1,0:T(8,128)(2,1)S(1)} %get-tuple-element.10.refs_0_, bf16[256,512]{1,0:T(8,128)(2,1)S(1)} %get-tuple-element.11.refs_1_, ...), custom_call_target="tpu_custom_call" | custom-call | tf_op jit(solution)/shard_map/pallas_call | solution.py:454

commit v4 on v3

--- a/solution.py
+++ b/solution.py
@@ -25,7 +25,7 @@
 MESH = pl.DeviceIdType.MESH
 F32 = jnp.float32
 BF16 = jnp.bfloat16
-OFFSETS = [(dz, dy) for dz in (2, 1, 3, 0) for dy in (2, 1, 3, 0) if (dz, dy) != (0, 0)]
+OFFSETS = [(dz, dy) for dy in (2, 1, 3, 0) for dz in (2, 1, 3, 0) if (dz, dy) != (0, 0)]
 
 
 def dot(a, b, ca, cb):
@@ -60,11 +60,11 @@
     normed_ref, dq_ref, dk_ref, dv_ref, dgain_ref,
     q_ref, k_ref, v_ref, y_ref, gain_ref, doc_ref,
     mask_ref, w_ref, att_ref, scaled_ref, dkl_ref, dvl_ref, ga_ref, qh_ref, kt_ref, vt_ref, qht_ref,
-    flag_src, flag_buf, keep_buf,
+    flag_src, flag_buf, keep_buf, fg_src, fg_buf,
     t_ref, tin_ref, pre_ref, tot_ref, totin_ref, carry_ref, sout_ref, s_ref,
     h_ref, hin_ref, htot_ref, htotin_ref, rout_ref, r_ref,
     ps_src, ps_buf, gy_src, gy_buf, gg_src, gg_buf, gt_src, gt_buf,
-    in_sem, ready, f_sem, ps_sem, gy_sem, gg_sem, gt_sem,
+    in_sem, ready, fus, fur, fds, fdr, f_sem, ps_sem, gy_sem, gg_sem, gt_sem,
     l1s, l1r, l2s, l2r, l3s, l3r, b1s, b1r, b2s, b2r, b3s, b3r,
 ):
     c = lax.axis_index("ctx")
@@ -129,15 +129,6 @@
     flag_src[...] = flag
     flag_buf[p] = flag
 
-    loads[0].wait()
-    loads[1].wait()
-    for h in range(LOCAL):
-        kt = k_ref[:, cols(h)] * tail_b
-        kt_ref[:, cols(h)] = kt
-        t_ref[part_of(h), share(h)] = dot(kt, v_ref[:, cols(h)], 0, 0).reshape(SHARE, SLAB, HEAD_DIM)
-    for s in range(PARTS):
-        tin_ref[s, p] = t_ref[s, p]
-
     pl.semaphore_wait(barrier, CUBE - 1 + HEAD_PEERS - 1 + g)
     for b in range(1, GROUPS):
         @pl.when(g - b >= 0)
@@ -161,8 +152,15 @@
         return remote(whole, whole, sem.at[0], sem.at[1], where)
 
     near = {"ctx": base + ranks[0]}
-    for s in range(PARTS):
-        spread(t_ref, tin_ref, l1s, l1r, s)
+    loads[0].wait()
+    loads[1].wait()
+    for h in range(LOCAL):
+        kt = k_ref[:, cols(h)] * tail_b
+        kt_ref[:, cols(h)] = kt
+        t_ref[part_of(h), share(h)] = dot(kt, v_ref[:, cols(h)], 0, 0).reshape(SHARE, SLAB, HEAD_DIM)
+        if h % PER == PER - 1:
+            tin_ref[part_of(h), p] = t_ref[part_of(h), p]
+            spread(t_ref, tin_ref, l1s, l1r, part_of(h))
 
     lane = lax.broadcasted_iota(jnp.int32, (ROWS, ROWS), 1)
     sub = lax.broadcasted_iota(jnp.int32, (ROWS, ROWS), 0)
@@ -194,21 +192,31 @@
     for i in range(CUBE):
         keep_buf[i] = keep
         keep = keep * (1.0 - flag_buf[i])
-    flag_tile = jnp.broadcast_to(1.0 - keep, (8, HEAD_DIM))
-    tot_ref[pl.ds(0, 8)] = flag_tile
-    htot_ref[pl.ds(0, 8)] = flag_tile
-
-    def span(s):
-        return pl.ds(0, 8 + SLAB) if s == 0 else rows_of(s)
+    fg_src[...] = 1.0 - keep
 
     def rows_of(s):
-        return pl.ds(8 + s * SLAB, SLAB)
+        return pl.ds(s * SLAB, SLAB)
 
     def up(b, s):
-        return remote(tot_ref.at[span(s)], totin_ref.at[g, span(s)], l2s.at[s, b], l2r.at[s, b], above(b))
+        return remote(
+            tot_ref.at[rows_of(s)], totin_ref.at[g, rows_of(s)], l2s.at[s, b], l2r.at[s, b], above(b)
+        )
 
     def down(b, s):
-        return remote(htot_ref.at[span(s)], htotin_ref.at[g, span(s)], b2s.at[s, b], b2r.at[s, b], below(b))
+        return remote(
+            htot_ref.at[rows_of(s)], htotin_ref.at[g, rows_of(s)], b2s.at[s, b], b2r.at[s, b], below(b)
+        )
+
+    def up_flag(b):
+        return remote(fg_src, fg_buf.at[g], fus.at[b], fur.at[b], above(b))
+
+    def down_flag(b):
+        return remote(fg_src, fg_buf.at[g], fds.at[b], fdr.at[b], below(b))
+
+    for b in range(1, GROUPS):
+        @pl.when(g - b >= 0)
+        def _():
+            down_flag(b).start()
 
     def fold(order, source, partial, total, s):
         acc = jnp.zeros((SLAB, HEAD_DIM), F32)
@@ -232,6 +240,7 @@
             def _():
                 if s == 0:
                     pl.semaphore_wait(ready.at[b], 1)
+                    up_flag(b).start()
                 up(b, s).start()
 
     for s in range(PARTS):
@@ -239,9 +248,11 @@
         for b in range(GROUPS - 1, 0, -1):
             @pl.when(g - b >= 0)
             def _():
+                if s == 0:
+                    up_flag(b).wait_recv()
                 up(b, s).wait_recv()
                 at = lax.rem(g + GROUPS - b, GROUPS)
-                hold = 1.0 - totin_ref[at, pl.ds(0, 1), :]
+                hold = 1.0 - fg_buf[at]
                 carry_ref[s] = totin_ref[at, rows_of(s), :] + hold * carry_ref[s]
 
         finish(pre_ref, sout_ref, s_ref, l3s, l3r, s)
@@ -343,9 +354,11 @@
         for b in range(GROUPS - 1, 0, -1):
             @pl.when(g + b < GROUPS)
             def _():
+                if s == 0:
+                    down_flag(b).wait_recv()
                 down(b, s).wait_recv()
                 at = lax.rem(g + b, GROUPS)
-                hold = 1.0 - htotin_ref[at, pl.ds(0, 1), :]
+                hold = 1.0 - fg_buf[at]
                 carry_ref[s] = htotin_ref[at, rows_of(s), :] + hold * carry_ref[s]
 
         finish(pre_ref, rout_ref, r_ref, b3s, b3r, s)
@@ -365,10 +378,14 @@
         for b in range(1, GROUPS):
             @pl.when(g + b < GROUPS)
             def _():
+                if s == 0:
+                    up_flag(b).wait_send()
                 up(b, s).wait_send()
 
             @pl.when(g - b >= 0)
             def _():
+                if s == 0:
+                    down_flag(b).wait_send()
                 down(b, s).wait_send()
 
     for h in range(LOCAL):
@@ -407,7 +424,7 @@
     vmem = pl.BlockSpec(memory_space=pltpu.VMEM)
     block = (ROWS, WIDE)
     pieces = (PARTS, CUBE, SLAB, HEAD_DIM)
-    total = (8 + PARTS * SLAB, HEAD_DIM)
+    total = (PARTS * SLAB, HEAD_DIM)
     dma = pltpu.SemaphoreType.DMA
     scratch = [pltpu.VMEM(block, BF16)] * 4
     scratch += [pltpu.VMEM((WIDE,), F32), pltpu.VMEM((ROWS,), jnp.int32)]
@@ -421,6 +438,8 @@
         pltpu.VMEM((1, HEAD_DIM), F32),
         pltpu.VMEM((CUBE, 1, HEAD_DIM), F32),
         pltpu.VMEM((CUBE, 1, HEAD_DIM), F32),
+        pltpu.VMEM((1, HEAD_DIM), F32),
+        pltpu.VMEM((GROUPS, 1, HEAD_DIM), F32),
     ]
     scratch += [pltpu.VMEM(pieces, F32)] * 3
     scratch += [
@@ -436,7 +455,8 @@
         pltpu.VMEM((HEAD_PEERS, 1, 2 * ROWS), F32),
     ]
     scratch += [pltpu.VMEM((1, WIDE), F32), pltpu.VMEM((GROUPS, 1, WIDE), F32)] * 3
-    scratch += [dma((6,)), pltpu.SemaphoreType.REGULAR((GROUPS,))] + [dma((2,))] * 5
+    scratch += [dma((6,)), pltpu.SemaphoreType.REGULAR((GROUPS,))]
+    scratch += [dma((GROUPS,))] * 4 + [dma((2,))] * 5
     one, pairs = dma((PARTS,)), dma((PARTS, GROUPS))
     scratch += [one, one, pairs, pairs, one, one] * 2
     shape = jax.ShapeDtypeStruct(block, BF16)

time: 61.9 us -> 61.9 us (level)
  the two profiles are of different devices: /device:TPU:1 before, /device:TPU:2 now
where the time goes in v4:
time: 61.9 us; the launch traced here: 61.7 us
  Pallas kernels  60.4 us (98%)
  between operations  1.29 us (2%)
    pallas_call x1, Pallas kernels, per_device(): pl.pallas_call(main_kernel, out_shape=(shape, shape, shape, shape, gains)...  59.4 us

profile of v4, /device:TPU:2, one launch (start us, length us, event | category | flops | bytes accessed | tf_op | source)
XLA Modules:
  0.0 61.7 jit_solution(15650944785298371972)
XLA Ops:
  1.3 59.4 %shard_map.110 = (bf16[256,512]{1,0:T(8,128)(2,1)S(1)}, bf16[256,512]{1,0:T(8,128)(2,1)S(1)}, bf16[256,512]{1,0:T(8,128)(2,1)S(1)}, bf16[256,512]{1,0:T(8,128)(2,1)S(1)}, f32[512]{0:T(512)S(1)}) custom-call(bf16[256,512]{1,0:T(8,128)(2,1)} %q_hbm.1, bf16[256,512]{1,0:T(8,128)(2,1)} %k_hbm.1, bf16[256,512]{1,0:T(8,128)(2,1)} %v_hbm.1, ...), custom_call_target="tpu_custom_call" | custom-call | tf_op jit(solution)/shard_map/pallas_call | solution.py:464
  60.7 1.0 %shard_map.111 = (bf16[256,512]{1,0:T(8,128)(2,1)}, bf16[256,512]{1,0:T(8,128)(2,1)}, bf16[256,512]{1,0:T(8,128)(2,1)}, bf16[256,512]{1,0:T(8,128)(2,1)}, f32[512]{0:T(512)}) custom-call(bf16[256,512]{1,0:T(8,128)(2,1)S(1)} %get-tuple-element.10.refs_0_, bf16[256,512]{1,0:T(8,128)(2,1)S(1)} %get-tuple-element.11.refs_1_, ...), custom_call_target="tpu_custom_call" | custom-call | tf_op jit(solution)/shard_map/pallas_call | solution.py:474
